TPU v7x, 256 devices: a whole 4x4x8 slice. The times are simulated.
256 devices in a mesh: expert: 16 (over x, y), edata: 16 (over z, core).
Axes of the slice: x: 4, y: 4, z: 8, core: 2. Of those that a mesh axis runs over, the one named last changes fastest.
Arguments:
- tokens: bfloat16 [1024, 7168], P(('expert', 'edata')), may hold values from -8 to 8
- routes: int32 [1024, 8], P(('expert', 'edata')), may hold values from 0 to 31, all different within a row; in each aligned block of 4 rows (0 to 3, 4 to 7, ...) at most 2 rows name the same one
- combine: bfloat16 [1024, 8], P(('expert', 'edata')), may hold values from 0.049804688 to 0.5
- w_gate: bfloat16 [32, 7168, 2048], P('expert', None, 'edata'), may hold values from -0.0625 to 0.0625
- w_up: bfloat16 [32, 7168, 2048], P('expert', None, 'edata')
- w_down: bfloat16 [32, 2048, 7168], P('expert', 'edata'), may hold values from -0.125 to 0.125
- past_amax: float32 [32], P('expert'), may hold values from 10 to 300
Outputs:
- layer_out: bfloat16 [1024, 7168], P(('expert', 'edata'))
- hidden_amax: float32 [32], P('expert')
Inputs may be any that keep to these rules, and one draw needn't show every extreme that they name: `routes`: each row names 8 different experts and every expert is named by some token. Among the 4 tokens of one device no expert is named more than 2 times, a bound that some block reaches.
All inputs are finite; a program needn't handle non-finite values.
Results may differ from a plain program's by a relative error of at most 0.018.
Values may be sent and summed in bfloat16 or wider, within the bound.
No kernel may reach another device: no remote copies, remote signals or barrier semaphores. Data moves between devices by JAX's collectives and lax.ppermute only.
A program may use at most 128 MiB of HBM per device.

v0:
```python
import jax
import jax.numpy as jnp
from jax import lax
from jax.sharding import PartitionSpec as P


quant_limit = 448.0
lane = 128
ring = 4


def per_device(tokens, routes, combine, w_gate, w_up, w_down, past_amax):
    groups = lax.axis_size("expert")
    members = lax.axis_size("edata")
    local_experts, model_width, hidden_units = w_gate.shape
    rows = tokens.shape[0]
    half = model_width // 2
    fan = local_experts * hidden_units
    core = lax.axis_index("edata") % 2
    group = lax.axis_index("expert")
    swap = [(i, i ^ 1) for i in range(members)]

    def pair(v):
        return lax.ppermute(v, "edata", swap)

    def shift(v, k, outer):
        moves = []
        for e in range(groups):
            for i in range(members):
                if (i % 2 == 0) == outer:
                    to = (e // ring + k) % ring * ring + e % ring
                else:
                    to = e // ring * ring + (e % ring + k) % ring
                moves.append((e * members + i, to * members + i))
        return lax.ppermute(v, ("expert", "edata"), moves)

    def inner(v, k):
        return shift(v, k, False)

    def outer(v, k):
        return shift(v, k, True)

    def small_gather(send, block):
        behind = send(block, 1)
        return [block, send(block, -1), send(behind, 1), behind]

    def ring_gather(send, low, high, ready):
        behind_low, ahead_high = send(low, 1), send(high, -1)
        behind_high, ahead_low = send(high, 1), send(low, -1)
        behind_low, ahead_high, ready = lax.optimization_barrier(
            (behind_low, ahead_high, ready)
        )
        far = [send(behind_low, 1), send(ahead_high, -1)]
        halves = [low, high, ahead_low, ahead_high, *far, behind_low, behind_high]
        return halves, ready

    def add(*parts):
        return sum(p.astype(jnp.float32) for p in parts).astype(jnp.bfloat16)

    def small_scatter(send, blocks):
        behind = send(blocks[3], -1)
        return add(blocks[0], behind, send(add(blocks[1], send(blocks[2], 1)), 1))

    def ring_scatter(send, blocks):
        cut = blocks[0].shape[0] // 2
        low, high = [b[:cut] for b in blocks], [b[cut:] for b in blocks]
        far_low, far_high = send(low[2], 1), send(high[2], -1)
        got_high, got_low = send(high[1], 1), send(low[3], -1)
        sums = lax.optimization_barrier((add(low[1], far_low), add(high[3], far_high)))
        last_low, last_high = send(sums[0], 1), send(sums[1], -1)
        return add(low[0], got_low, last_low), add(high[0], got_high, last_high)

    lanes = jnp.arange(lane, dtype=jnp.int32)
    hits = routes[:, :, None] == lanes[None, None, :]
    weights = jnp.sum(jnp.where(hits, combine.astype(jnp.float32)[:, :, None], 0.0), axis=1)
    weights = weights.astype(jnp.bfloat16)

    pieces = jnp.stack(
        [
            jnp.concatenate([tokens[:, :half], weights], axis=1),
            jnp.concatenate([tokens[:, half:], weights], axis=1),
        ]
    )
    outgoing = jnp.broadcast_to(pieces[None], (members // 2, 2, rows, half + lane))
    outgoing = outgoing.reshape(members, rows, half + lane)
    line = lax.all_to_all(outgoing, "edata", split_axis=0, concat_axis=0, tiled=True)
    line = line.reshape(members * rows, half + lane)
    line_rows = members * rows

    plane = small_gather(inner, line)
    low, high = [jnp.concatenate(plane[k : k + 2], axis=0) for k in (0, 2)]
    low, high, w_gate, w_up, w_down = lax.optimization_barrier(
        (low, high, w_gate, w_up, w_down)
    )

    def joined_half(side):
        cut = [
            lax.dynamic_slice_in_dim(w, side * half, half, axis=1)[j]
            for w in (w_gate, w_up)
            for j in range(local_experts)
        ]
        return jnp.concatenate(cut, axis=1)

    def down_half(side):
        return lax.dynamic_slice_in_dim(w_down, side * half, half, axis=2).reshape(fan, half)

    w_own = joined_half(core)
    other_half = joined_half(1 - core)
    other_down = down_half(1 - core)
    w_other = pair(other_half)
    down_got = pair(other_down)
    down_own = down_half(core)

    blocks, (w_own, down_own, down_got) = ring_gather(outer, low, high, (w_own, down_own, down_got))
    w_out = jnp.concatenate([down_own, down_got], axis=0)
    everyone = jnp.concatenate(blocks, axis=0)

    def project(w):
        return jnp.dot(everyone[:, :half], w, preferred_element_type=jnp.float32)

    def swapped(v):
        v = v.reshape(ring, ring, line_rows, v.shape[1])
        return v.swapaxes(0, 1).reshape(ring * ring * line_rows, v.shape[3])

    unit_expert = jnp.arange(fan, dtype=jnp.int32) // hidden_units
    spread = (lanes[:, None] == group * local_experts + unit_expert[None, :]).astype(jnp.bfloat16)
    quant_gain = jnp.repeat(quant_limit / past_amax, hidden_units)
    dequant = jnp.repeat(past_amax / quant_limit, hidden_units)

    got = swapped(pair(project(w_other)))
    weight = jnp.dot(everyone[:, half:], spread, preferred_element_type=jnp.float32)
    both_proj = lax.optimization_barrier(project(w_own)) + got
    gate_proj = both_proj[:, :fan]
    up_proj = both_proj[:, fan:]
    hidden = jax.nn.silu(gate_proj) * up_proj
    peaks = jnp.max(jnp.where(weight > 0.0, jnp.abs(hidden), 0.0), axis=0)
    peaks = jnp.pad(peaks.reshape(local_experts, hidden_units), ((0, 0), (0, lane - hidden_units)))
    clipped = jnp.clip(hidden * quant_gain[None, :], -quant_limit, quant_limit)
    scaled = (clipped * (weight * dequant[None, :])).astype(jnp.bfloat16)
    both = jnp.concatenate([scaled, swapped(pair(scaled))], axis=1)
    down = jnp.dot(both, w_out, preferred_element_type=jnp.float32).astype(jnp.bfloat16)

    low, high = ring_scatter(outer, jnp.split(down, ring))
    line_sum = small_scatter(inner, [*jnp.split(low, 2), *jnp.split(high, 2)])

    def split(v):
        top = lax.reduce_precision(v, 8, 7)
        return jnp.concatenate([top, v - top], axis=0).astype(jnp.bfloat16)

    def joined(v):
        v = v.astype(jnp.float32)
        return v[:local_experts] + v[local_experts : 2 * local_experts]

    tail = jnp.pad(split(peaks), ((0, rows - 2 * local_experts), (0, 0)))
    tail = jnp.broadcast_to(tail[None], (members, rows, lane))
    message = line_sum.reshape(members, rows, half)
    message = jnp.concatenate([message, tail], axis=2)
    back = lax.all_to_all(message, "edata", split_axis=0, concat_axis=0, tiled=True)
    hidden_amax = jnp.max(jax.vmap(joined)(back[:, :, half:]), axis=(0, 2))
    total = jnp.sum(
        back[:, :, :half].reshape(members // 2, 2, rows, half).astype(jnp.float32), axis=0
    )
    layer_out = jnp.concatenate([total[0], total[1]], axis=1).astype(jnp.bfloat16)
    return (layer_out, hidden_amax)


def solution(mesh):
    return jax.shard_map(
        per_device,
        mesh=mesh,
        in_specs=(
            P(("expert", "edata"), None),
            P(("expert", "edata"), None),
            P(("expert", "edata"), None),
            P("expert", None, "edata"),
            P("expert", None, "edata"),
            P("expert", "edata", None),
            P("expert"),
        ),
        out_specs=(P(("expert", "edata"), None), P("expert")),
        check_vma=False,
    )
```

profile of v0, /device:TPU:2, one launch (start us, length us, event | category | flops | bytes accessed | tf_op | source)
XLA Modules:
  0.0 186.5 jit_solution(14538192259820051763)
XLA Ops:
  0.6 0.8 fusion.21
  1.4 0.7 convert_element_type.91
  2.1 0.8 select_reduce_fusion.1
  3.1 23.4 %all_to_all.10 = bf16[16,4,3712]{2,1,0:T(4,128)(2,1)S(1)} all-to-all(bf16[16,4,3712]{2,1,0:T(4,128)(2,1)S(1)} %bitcast.47), channel_id=1, replica_groups=mesh['expert'=16,'edata'=16] {'edata'}, dimensions={0} | all-to-all | bytes 950272 | tf_op jit(solution)/shard_map/all_to_all | solution.py:86
  26.6 1.7 collective-permute-start.1
  28.3 1.7 collective-permute-start
  30.0 6.6 %collective-permute-done.1 = bf16[64,3712]{1,0:T(8,128)(2,1)S(1)} collective-permute-done((bf16[64,3712]{1,0:T(8,128)(2,1)S(1)}, bf16[64,3712]{1,0:T(8,128)(2,1)S(1)}, u32[]{:S(2)}, u32[]{:S(2)}) %collective-permute-start.1) | collective-permute-done | bytes 475168 | tf_op jit(solution)/shard_map/ppermute | solution.py:35
  36.6 0.4 collective-permute-start.2
  37.0 9.4 %collective-permute-done.2 = bf16[64,3712]{1,0:T(8,128)(2,1)S(1)} collective-permute-done((bf16[64,3712]{1,0:T(8,128)(2,1)S(1)}, bf16[64,3712]{1,0:T(8,128)(2,1)S(1)}, u32[]{:S(2)}, u32[]{:S(2)}) %collective-permute-start.2) | collective-permute-done | bytes 475168 | tf_op jit(solution)/shard_map/ppermute | solution.py:35
  46.6 1.6 collective-permute-start.4
  48.1 0.5 collective-permute-start.3
  48.7 1.5 constant_dynamic-slice_fusion
  50.1 1.7 collective-permute-start.5
  51.9 0.5 dynamic-slice_bitcast_fusion.1
  52.3 0.4 pad_maximum_fusion.1
  52.9 2.1 %pad_maximum_fusion = bf16[3584,512]{1,0:T(8,128)(2,1)} fusion(bf16[3584,128]{1,0:T(8,128)(2,1)S(1)} %get-tuple-element.41, bf16[3584,128]{1,0:T(8,128)(2,1)S(1)} %get-tuple-element.39, bf16[3584,128]{1,0:T(8,128)(2,1)S(1)} %get-tuple-element.60, bf16[3584,128]{1,0:T(8,128)(2,1)S(1)} %get-tuple-element.62), kind=kLoop, calls=%fused_computation.5 | loop fusion | flops 14680064 | bytes 7340032 | tf_op jit(solution)/shard_map/concatenate | solution.py:102
  55.1 5.3 %collective-permute-done.4 = bf16[128,3712]{1,0:T(8,128)(2,1)S(1)} collective-permute-done((bf16[128,3712]{1,0:T(8,128)(2,1)S(1)}, bf16[128,3712]{1,0:T(8,128)(2,1)S(1)}, u32[]{:S(2)}, u32[]{:S(2)}) %collective-permute-start.4) | collective-permute-done | bytes 950304 | tf_op jit(solution)/shard_map/ppermute | solution.py:35
  60.4 1.5 collective-permute-start.9
  61.9 10.2 %collective-permute-done.5 = bf16[128,3712]{1,0:T(8,128)(2,1)S(1)} collective-permute-done((bf16[128,3712]{1,0:T(8,128)(2,1)S(1)}, bf16[128,3712]{1,0:T(8,128)(2,1)S(1)}, u32[]{:S(2)}, u32[]{:S(2)}) %collective-permute-start.5) | collective-permute-done | bytes 950304 | tf_op jit(solution)/shard_map/ppermute | solution.py:35
  72.1 1.2 collective-permute-start.7
  73.4 1.1 collective-permute-start.8
  74.7 11.1 %collective-permute-done.7 = bf16[128,3712]{1,0:T(8,128)(2,1)S(1)} collective-permute-done((bf16[128,3712]{1,0:T(8,128)(2,1)S(1)}, bf16[128,3712]{1,0:T(8,128)(2,1)S(1)}, u32[]{:S(2)}, u32[]{:S(2)}) %collective-permute-start.7) | collective-permute-done | bytes 950304 | tf_op jit(solution)/shard_map/ppermute | solution.py:35
  85.9 1.4 collective-permute-done.8
  87.8 5.4 %fusion = f32[1024,512]{1,0:T(8,128)} fusion(bf16[3584,512]{1,0:T(8,128)(2,1)S(1)} %collective-permute-done.10, bf16[1024,3712]{1,0:T(8,128)(2,1)S(1)} %constant_dynamic-update-slice_fusion), kind=kOutput, calls=%fused_computation.1 | convolution fusion | flops 3758096384 | bytes 13107200 | tf_op jit(solution)/shard_map/dot_general | solution.py:119
  93.3 7.3 %fusion.2 = f32[1024,512]{1,0:T(8,128)S(1)} fusion(bf16[3584,512]{1,0:T(8,128)(2,1)} %pad_maximum_fusion, bf16[1024,3712]{1,0:T(8,128)(2,1)} %copy-done.4), kind=kOutput, calls=%fused_computation.3 | convolution fusion | flops 3758096384 | bytes 13107200 | tf_op jit(solution)/shard_map/dot_general | solution.py:119
  100.8 0.5 bitcast_add_fusion
  101.3 1.8 multiply_convert_fusion
  103.1 0.6 collective-permute-start.12
  103.7 1.5 collective-permute-done.12
  105.3 4.2 %convolution_convert_fusion = bf16[1024,3584]{1,0:T(8,128)(2,1)S(1)} fusion(bf16[256,3584]{1,0:T(8,128)(2,1)S(1)} %copy-done.6, bf16[256,3584]{1,0:T(8,128)(2,1)S(1)} %bitcast.49, bf16[1024,256]{1,0:T(8,128)(2,1)S(1)} %bitcast.51, bf16[1024,256]{1,0:T(8,128)(2,1)S(1)} %get-tuple-element.44), kind=kOutput, calls=%fused_computation | convolution fusion | flops 3771203584 | bytes 12058624 | tf_op jit(solution)/shard_map/dot_general | solution.py:141
  109.7 1.8 collective-permute-start.14
  111.5 0.3 collective-permute-start.15
  111.8 2.1 %collective-permute-start.13 = (bf16[128,3584]{1,0:T(8,128)(2,1)S(1)}, bf16[128,3584]{1,0:T(8,128)(2,1)S(1)}, u32[]{:S(2)}, u32[]{:S(2)}) collective-permute-start(bf16[128,3584]{1,0:T(8,128)(2,1)S(1)} %get-tuple-element.28), channel_id=1, source_target_pairs={{0,192},{1,49},{2,194},{3,51},{4,196},{5,53},{6,198},{7,55},{8,200... | collective-permute-start | bytes 2752520 | tf_op jit(solution)/shard_map/ppermute | solution.py:35
  113.9 9.3 %collective-permute-done.14 = bf16[128,3584]{1,0:T(8,128)(2,1)S(1)} collective-permute-done((bf16[128,3584]{1,0:T(8,128)(2,1)S(1)}, bf16[128,3584]{1,0:T(8,128)(2,1)S(1)}, u32[]{:S(2)}, u32[]{:S(2)}) %collective-permute-start.14) | collective-permute-done | bytes 917536 | tf_op jit(solution)/shard_map/ppermute | solution.py:35
  123.2 1.7 collective-permute-done.15
  124.9 0.6 add_convert_fusion.2
  125.5 1.8 collective-permute-start.16
  127.2 0.5 collective-permute-start.18
  127.8 6.9 %collective-permute-done.13 = bf16[128,3584]{1,0:T(8,128)(2,1)S(1)} collective-permute-done((bf16[128,3584]{1,0:T(8,128)(2,1)S(1)}, bf16[128,3584]{1,0:T(8,128)(2,1)S(1)}, u32[]{:S(2)}, u32[]{:S(2)}) %collective-permute-start.13) | collective-permute-done | bytes 917536 | tf_op jit(solution)/shard_map/ppermute | solution.py:35
  134.7 8.1 %collective-permute-done.16 = bf16[128,3584]{1,0:T(8,128)(2,1)S(1)} collective-permute-done((bf16[128,3584]{1,0:T(8,128)(2,1)S(1)}, bf16[128,3584]{1,0:T(8,128)(2,1)S(1)}, u32[]{:S(2)}, u32[]{:S(2)}) %collective-permute-start.16) | collective-permute-done | bytes 917536 | tf_op jit(solution)/shard_map/ppermute | solution.py:35
  142.9 1.7 collective-permute-done.18
  144.6 0.7 add_convert_fusion.1
  145.4 3.2 %collective-permute-start.19 = (bf16[64,3584]{1,0:T(8,128)(2,1)S(1)}, bf16[64,3584]{1,0:T(8,128)(2,1)S(1)}, u32[]{:S(2)}, u32[]{:S(2)}) collective-permute-start(bf16[64,3584]{1,0:T(8,128)(2,1)S(1)} %get-tuple-element.46), channel_id=1, source_target_pairs={{0,48},{1,193},{2,50},{3,195},{4,52},{5,197},{6,54},{7,199},{8,56}... | collective-permute-start | bytes 1376264 | tf_op jit(solution)/shard_map/ppermute | solution.py:35
  148.6 6.5 %collective-permute-done.20 = bf16[64,3584]{1,0:T(8,128)(2,1)S(1)} collective-permute-done((bf16[64,3584]{1,0:T(8,128)(2,1)S(1)}, bf16[64,3584]{1,0:T(8,128)(2,1)S(1)}, u32[]{:S(2)}, u32[]{:S(2)}) %collective-permute-start.20) | collective-permute-done | bytes 458784 | tf_op jit(solution)/shard_map/ppermute | solution.py:35
  155.3 9.6 %collective-permute-done.21 = bf16[64,3584]{1,0:T(8,128)(2,1)S(1)} collective-permute-done((bf16[64,3584]{1,0:T(8,128)(2,1)S(1)}, bf16[64,3584]{1,0:T(8,128)(2,1)S(1)}, u32[]{:S(2)}, u32[]{:S(2)}) %collective-permute-start.21) | collective-permute-done | bytes 458784 | tf_op jit(solution)/shard_map/ppermute | solution.py:35
  165.5 19.3 %all_to_all.11 = bf16[16,4,3712]{2,1,0:T(4,128)(2,1)S(1)} all-to-all(bf16[16,4,3712]{2,1,0:T(4,128)(2,1)S(1)} %pad_maximum_fusion.4), channel_id=1, replica_groups=mesh['expert'=16,'edata'=16] {'edata'}, dimensions={0} | all-to-all | bytes 950272 | tf_op jit(solution)/shard_map/all_to_all | solution.py:158
  185.2 0.6 fusion.15
  185.9 0.6 pad_maximum_fusion.6
  (62 shorter events, 3.2 us)
Async XLA Ops:
  26.6 9.9 %collective-permute-start.1 = (bf16[64,3712]{1,0:T(8,128)(2,1)S(1)}, bf16[64,3712]{1,0:T(8,128)(2,1)S(1)}, u32[]{:S(2)}, u32[]{:S(2)}) collective-permute-start(bf16[64,3712]{1,0:T(8,128)(2,1)S(1)} %reshape.73), channel_id=1, source_target_pairs={{0,16},{1,65},{2,18},{3,67},{4,20},{5,69},{6,22},{7,71},{8,24},{9,... | collective-permute-start | bytes 1425416 | tf_op jit(solution)/shard_map/ppermute | solution.py:35
  28.3 8.7 %collective-permute-start = (bf16[64,3712]{1,0:T(8,128)(2,1)S(1)}, bf16[64,3712]{1,0:T(8,128)(2,1)S(1)}, u32[]{:S(2)}, u32[]{:S(2)}) collective-permute-start(bf16[64,3712]{1,0:T(8,128)(2,1)S(1)} %reshape.73), channel_id=1, source_target_pairs={{0,48},{1,193},{2,50},{3,195},{4,52},{5,197},{6,54},{7,199},{8,56}... | collective-permute-start | bytes 1425416 | tf_op jit(solution)/shard_map/ppermute | solution.py:35
  36.6 9.9 %collective-permute-start.2 = (bf16[64,3712]{1,0:T(8,128)(2,1)S(1)}, bf16[64,3712]{1,0:T(8,128)(2,1)S(1)}, u32[]{:S(2)}, u32[]{:S(2)}) collective-permute-start(bf16[64,3712]{1,0:T(8,128)(2,1)S(1)} %collective-permute-done.1), channel_id=1, source_target_pairs={{0,16},{1,65},{2,18},{3,67},{4,20},{5,69},{6,22},{7,71},{8,24},{9,... | collective-permute-start | bytes 1425416 | tf_op jit(solution)/shard_map/ppermute | solution.py:35
  37.0 11.7 %copy-start = (bf16[2,128,7168]{2,1,0:T(8,128)(2,1)S(1)}, bf16[2,128,7168]{2,1,0:T(8,128)(2,1)}, u32[]{:S(2)}) copy-start(bf16[2,128,7168]{2,1,0:T(8,128)(2,1)} %param.12) | copy-start | bytes 11010052
  46.5 5.3 %copy-start.1 = (bf16[2,7168,128]{2,1,0:T(8,128)(2,1)S(1)}, bf16[2,7168,128]{2,1,0:T(8,128)(2,1)}, u32[]{:S(2)}) copy-start(bf16[2,7168,128]{2,1,0:T(8,128)(2,1)} %param.11) | copy-start | bytes 11010052
  46.5 5.3 %copy-start.2 = (bf16[2,7168,128]{2,1,0:T(8,128)(2,1)S(1)}, bf16[2,7168,128]{2,1,0:T(8,128)(2,1)}, u32[]{:S(2)}) copy-start(bf16[2,7168,128]{2,1,0:T(8,128)(2,1)} %param.10) | copy-start | bytes 11010052
  46.6 13.8 %collective-permute-start.4 = (bf16[128,3712]{1,0:T(8,128)(2,1)S(1)}, bf16[128,3712]{1,0:T(8,128)(2,1)S(1)}, u32[]{:S(2)}, u32[]{:S(2)}) collective-permute-start(bf16[128,3712]{1,0:T(8,128)(2,1)S(1)} %pad_maximum_fusion.2), channel_id=1, source_target_pairs={{0,64},{1,17},{2,66},{3,19},{4,68},{5,21},{6,70},{7,23},{8,72},{9,... | collective-permute-start | bytes 2850824 | tf_op jit(solution)/shard_map/ppermute | solution.py:35
  48.1 26.3 %collective-permute-start.3 = (bf16[128,3712]{1,0:T(8,128)(2,1)S(1)}, bf16[128,3712]{1,0:T(8,128)(2,1)S(1)}, u32[]{:S(2)}, u32[]{:S(2)}) collective-permute-start(bf16[128,3712]{1,0:T(8,128)(2,1)S(1)} %pad_maximum_fusion.2), channel_id=1, source_target_pairs={{0,192},{1,49},{2,194},{3,51},{4,196},{5,53},{6,198},{7,55},{8,200... | collective-permute-start | bytes 2850824 | tf_op jit(solution)/shard_map/ppermute | solution.py:35
  50.1 21.9 %collective-permute-start.6 = (bf16[256,3584]{1,0:T(8,128)(2,1)S(1)}, bf16[256,3584]{1,0:T(8,128)(2,1)S(1)}, u32[]{:S(2)}, u32[]{:S(2)}) collective-permute-start(bf16[256,3584]{1,0:T(8,128)(2,1)S(1)} %bitcast.50), channel_id=1, source_target_pairs={{0,1},{1,0},{2,3},{3,2},{4,5},{5,4},{6,7},{7,6},{8,9},{9,8},{10,11... | collective-permute-start | bytes 5505032 | tf_op jit(solution)/shard_map/ppermute | solution.py:24
  50.1 21.9 %collective-permute-start.5 = (bf16[128,3712]{1,0:T(8,128)(2,1)S(1)}, bf16[128,3712]{1,0:T(8,128)(2,1)S(1)}, u32[]{:S(2)}, u32[]{:S(2)}) collective-permute-start(bf16[128,3712]{1,0:T(8,128)(2,1)S(1)} %pad_maximum_fusion.3), channel_id=1, source_target_pairs={{0,192},{1,49},{2,194},{3,51},{4,196},{5,53},{6,198},{7,55},{8,200... | collective-permute-start | bytes 2850824 | tf_op jit(solution)/shard_map/ppermute | solution.py:35
  52.8 35.0 %collective-permute-start.10 = (bf16[3584,512]{1,0:T(8,128)(2,1)S(1)}, bf16[3584,512]{1,0:T(8,128)(2,1)S(1)}, u32[]{:S(2)}, u32[]{:S(2)}) collective-permute-start(bf16[3584,512]{1,0:T(8,128)(2,1)S(1)} %pad_maximum_fusion.1), channel_id=1, source_target_pairs={{0,1},{1,0},{2,3},{3,2},{4,5},{5,4},{6,7},{7,6},{8,9},{9,8},{10,11... | collective-permute-start | bytes 11010056 | tf_op jit(solution)/shard_map/ppermute | solution.py:24
  60.4 27.2 %collective-permute-start.9 = (bf16[128,3712]{1,0:T(8,128)(2,1)S(1)}, bf16[128,3712]{1,0:T(8,128)(2,1)S(1)}, u32[]{:S(2)}, u32[]{:S(2)}) collective-permute-start(bf16[128,3712]{1,0:T(8,128)(2,1)S(1)} %pad_maximum_fusion.3), channel_id=1, source_target_pairs={{0,64},{1,17},{2,66},{3,19},{4,68},{5,21},{6,70},{7,23},{8,72},{9,... | collective-permute-start | bytes 2850824 | tf_op jit(solution)/shard_map/ppermute | solution.py:35
  72.1 13.9 %copy-start.5 = (bf16[256,3584]{1,0:T(8,128)(2,1)}, bf16[256,3584]{1,0:T(8,128)(2,1)S(1)}, u32[]{:S(2)}) copy-start(bf16[256,3584]{1,0:T(8,128)(2,1)S(1)} %collective-permute-done.6) | copy-start | bytes 5505028
  72.1 13.7 %collective-permute-start.7 = (bf16[128,3712]{1,0:T(8,128)(2,1)S(1)}, bf16[128,3712]{1,0:T(8,128)(2,1)S(1)}, u32[]{:S(2)}, u32[]{:S(2)}) collective-permute-start(bf16[128,3712]{1,0:T(8,128)(2,1)S(1)} %collective-permute-done.4), channel_id=1, source_target_pairs={{0,64},{1,17},{2,66},{3,19},{4,68},{5,21},{6,70},{7,23},{8,72},{9,... | collective-permute-start | bytes 2850824 | tf_op jit(solution)/shard_map/ppermute | solution.py:35
  73.4 14.0 %collective-permute-start.8 = (bf16[128,3712]{1,0:T(8,128)(2,1)S(1)}, bf16[128,3712]{1,0:T(8,128)(2,1)S(1)}, u32[]{:S(2)}, u32[]{:S(2)}) collective-permute-start(bf16[128,3712]{1,0:T(8,128)(2,1)S(1)} %collective-permute-done.5), channel_id=1, source_target_pairs={{0,192},{1,49},{2,194},{3,51},{4,196},{5,53},{6,198},{7,55},{8,200... | collective-permute-start | bytes 2850824 | tf_op jit(solution)/shard_map/ppermute | solution.py:35
  87.7 5.5 %copy-start.4 = (bf16[1024,3712]{1,0:T(8,128)(2,1)}, bf16[1024,3712]{1,0:T(8,128)(2,1)S(1)}, u32[]{:S(2)}) copy-start(bf16[1024,3712]{1,0:T(8,128)(2,1)S(1)} %constant_dynamic-update-slice_fusion) | copy-start | bytes 22806532
  87.8 5.5 %copy-start.7 = (f32[2]{0:T(128)S(1)}, f32[2]{0:T(128)}, u32[]{:S(2)}) copy-start(f32[2]{0:T(128)} %param.13) | copy-start | bytes 28
  93.2 7.4 %collective-permute-start.11 = (f32[1024,512]{1,0:T(8,128)}, f32[1024,512]{1,0:T(8,128)S(1)}, u32[]{:S(2)}, u32[]{:S(2)}) collective-permute-start(f32[1024,512]{1,0:T(8,128)} %fusion), channel_id=1, source_target_pairs={{0,1},{1,0},{2,3},{3,2},{4,5},{5,4},{6,7},{7,6},{8,9},{9,8},{10,11... | collective-permute-start | bytes 6291464 | tf_op jit(solution)/shard_map/ppermute | solution.py:24
  101.3 3.9 %copy-start.3 = (bf16[2,128,3584]{2,1,0:T(8,128)(2,1)S(1)}, bf16[2,128,3584]{2,1,0:T(8,128)(2,1)}, u32[]{:S(2)}) copy-start(bf16[2,128,3584]{2,1,0:T(8,128)(2,1)} %get-tuple-element.43) | copy-start | bytes 5505028
  101.3 3.9 %copy-start.6 = (bf16[256,3584]{1,0:T(8,128)(2,1)S(1)}, bf16[256,3584]{1,0:T(8,128)(2,1)}, u32[]{:S(2)}) copy-start(bf16[256,3584]{1,0:T(8,128)(2,1)} %copy-done.5) | copy-start | bytes 5505028
  103.1 2.1 %collective-permute-start.12 = (bf16[1024,256]{1,0:T(8,128)(2,1)S(1)}, bf16[1024,256]{1,0:T(8,128)(2,1)S(1)}, u32[]{:S(2)}, u32[]{:S(2)}) collective-permute-start(bf16[1024,256]{1,0:T(8,128)(2,1)S(1)} %get-tuple-element.44), channel_id=1, source_target_pairs={{0,1},{1,0},{2,3},{3,2},{4,5},{5,4},{6,7},{7,6},{8,9},{9,8},{10,11... | collective-permute-start | bytes 1572872 | tf_op jit(solution)/shard_map/ppermute | solution.py:24
  109.7 13.5 %collective-permute-start.14 = (bf16[128,3584]{1,0:T(8,128)(2,1)S(1)}, bf16[128,3584]{1,0:T(8,128)(2,1)S(1)}, u32[]{:S(2)}, u32[]{:S(2)}) collective-permute-start(bf16[128,3584]{1,0:T(8,128)(2,1)S(1)} %get-tuple-element.31), channel_id=1, source_target_pairs={{0,64},{1,17},{2,66},{3,19},{4,68},{5,21},{6,70},{7,23},{8,72},{9,... | collective-permute-start | bytes 2752520 | tf_op jit(solution)/shard_map/ppermute | solution.py:35
  111.5 13.4 %collective-permute-start.15 = (bf16[128,3584]{1,0:T(8,128)(2,1)S(1)}, bf16[128,3584]{1,0:T(8,128)(2,1)S(1)}, u32[]{:S(2)}, u32[]{:S(2)}) collective-permute-start(bf16[128,3584]{1,0:T(8,128)(2,1)S(1)} %get-tuple-element.30), channel_id=1, source_target_pairs={{0,192},{1,49},{2,194},{3,51},{4,196},{5,53},{6,198},{7,55},{8,200... | collective-permute-start | bytes 2752520 | tf_op jit(solution)/shard_map/ppermute | solution.py:35
  111.8 22.9 %collective-permute-start.13 = (bf16[128,3584]{1,0:T(8,128)(2,1)S(1)}, bf16[128,3584]{1,0:T(8,128)(2,1)S(1)}, u32[]{:S(2)}, u32[]{:S(2)}) collective-permute-start(bf16[128,3584]{1,0:T(8,128)(2,1)S(1)} %get-tuple-element.28), channel_id=1, source_target_pairs={{0,192},{1,49},{2,194},{3,51},{4,196},{5,53},{6,198},{7,55},{8,200... | collective-permute-start | bytes 2752520 | tf_op jit(solution)/shard_map/ppermute | solution.py:35
  113.9 20.9 %collective-permute-start.17 = (bf16[128,3584]{1,0:T(8,128)(2,1)S(1)}, bf16[128,3584]{1,0:T(8,128)(2,1)S(1)}, u32[]{:S(2)}, u32[]{:S(2)}) collective-permute-start(bf16[128,3584]{1,0:T(8,128)(2,1)S(1)} %get-tuple-element.29), channel_id=1, source_target_pairs={{0,64},{1,17},{2,66},{3,19},{4,68},{5,21},{6,70},{7,23},{8,72},{9,... | collective-permute-start | bytes 2752520 | tf_op jit(solution)/shard_map/ppermute | solution.py:35
  125.5 17.4 %collective-permute-start.16 = (bf16[128,3584]{1,0:T(8,128)(2,1)S(1)}, bf16[128,3584]{1,0:T(8,128)(2,1)S(1)}, u32[]{:S(2)}, u32[]{:S(2)}) collective-permute-start(bf16[128,3584]{1,0:T(8,128)(2,1)S(1)} %get-tuple-element.24), channel_id=1, source_target_pairs={{0,64},{1,17},{2,66},{3,19},{4,68},{5,21},{6,70},{7,23},{8,72},{9,... | collective-permute-start | bytes 2752520 | tf_op jit(solution)/shard_map/ppermute | solution.py:35
  127.2 17.3 %collective-permute-start.18 = (bf16[128,3584]{1,0:T(8,128)(2,1)S(1)}, bf16[128,3584]{1,0:T(8,128)(2,1)S(1)}, u32[]{:S(2)}, u32[]{:S(2)}) collective-permute-start(bf16[128,3584]{1,0:T(8,128)(2,1)S(1)} %get-tuple-element.25), channel_id=1, source_target_pairs={{0,192},{1,49},{2,194},{3,51},{4,196},{5,53},{6,198},{7,55},{8,200... | collective-permute-start | bytes 2752520 | tf_op jit(solution)/shard_map/ppermute | solution.py:35
  145.3 9.8 %collective-permute-start.20 = (bf16[64,3584]{1,0:T(8,128)(2,1)S(1)}, bf16[64,3584]{1,0:T(8,128)(2,1)S(1)}, u32[]{:S(2)}, u32[]{:S(2)}) collective-permute-start(bf16[64,3584]{1,0:T(8,128)(2,1)S(1)} %get-tuple-element.47), channel_id=1, source_target_pairs={{0,16},{1,65},{2,18},{3,67},{4,20},{5,69},{6,22},{7,71},{8,24},{9,... | collective-permute-start | bytes 1376264 | tf_op jit(solution)/shard_map/ppermute | solution.py:35
  145.4 9.9 %collective-permute-start.19 = (bf16[64,3584]{1,0:T(8,128)(2,1)S(1)}, bf16[64,3584]{1,0:T(8,128)(2,1)S(1)}, u32[]{:S(2)}, u32[]{:S(2)}) collective-permute-start(bf16[64,3584]{1,0:T(8,128)(2,1)S(1)} %get-tuple-element.46), channel_id=1, source_target_pairs={{0,48},{1,193},{2,50},{3,195},{4,52},{5,197},{6,54},{7,199},{8,56}... | collective-permute-start | bytes 1376264 | tf_op jit(solution)/shard_map/ppermute | solution.py:35
  155.2 9.8 %collective-permute-start.21 = (bf16[64,3584]{1,0:T(8,128)(2,1)S(1)}, bf16[64,3584]{1,0:T(8,128)(2,1)S(1)}, u32[]{:S(2)}, u32[]{:S(2)}) collective-permute-start(bf16[64,3584]{1,0:T(8,128)(2,1)S(1)} %add_convert_fusion.5), channel_id=1, source_target_pairs={{0,16},{1,65},{2,18},{3,67},{4,20},{5,69},{6,22},{7,71},{8,24},{9,... | collective-permute-start | bytes 1376264 | tf_op jit(solution)/shard_map/ppermute | solution.py:35
where the time goes:
time: 190 us; the launch traced here: 187 us
  waiting for transfers between devices  89.5 us (47%)
  blocking collectives  42.8 us (23%)
  starting transfers between devices  21.8 us (11%)
  matrix products  18.7 us (10%)
  other arithmetic  8.02 us (4%)
  local copies, waits for them, and re-layouts  4.73 us (2%)
    ppermute x18, waiting for transfers between devices, shift(): return lax.ppermute(v, ('expert', 'edata'), moves)  87.9 us
    all_to_all x1, blocking collectives, per_device(): lax.all_to_all(outgoing, 'edata', split_axis=0, concat_axis=0, tiled=True)  23.4 us
    ppermute x18, starting transfers between devices, shift(): return lax.ppermute(v, ('expert', 'edata'), moves)  21.2 us
    all_to_all x1, blocking collectives, per_device(): lax.all_to_all(message, 'edata', split_axis=0, concat_axis=0, tiled=True)  19.3 us
    dot_general x2, matrix products, project(): return jnp.dot(everyone[:, :half], w, preferred_element_type=jnp.float32)  12.7 us
    dot_general x1, matrix products, per_device(): jnp.dot(both, w_out, preferred_element_type=jnp.float32)  4.19 us
  transfers between devices with their start and end apart: 22, of which 14 were waited for; matrix products, arithmetic and copies ran while one was open for 7% of the time, Pallas kernels for 0%

commit v1 on v0

--- a/solution.py
+++ b/solution.py
@@ -40,35 +40,26 @@
     def outer(v, k):
         return shift(v, k, True)
 
-    def small_gather(send, block):
-        behind = send(block, 1)
-        return [block, send(block, -1), send(behind, 1), behind]
-
-    def ring_gather(send, low, high, ready):
+    def ring_gather(send, low, high, ready=()):
         behind_low, ahead_high = send(low, 1), send(high, -1)
         behind_high, ahead_low = send(high, 1), send(low, -1)
         behind_low, ahead_high, ready = lax.optimization_barrier(
             (behind_low, ahead_high, ready)
         )
         far = [send(behind_low, 1), send(ahead_high, -1)]
-        halves = [low, high, ahead_low, ahead_high, *far, behind_low, behind_high]
+        halves = [low, high, ahead_low, ahead_high, behind_low, behind_high, *far]
         return halves, ready
 
     def add(*parts):
         return sum(p.astype(jnp.float32) for p in parts).astype(jnp.bfloat16)
 
-    def small_scatter(send, blocks):
-        behind = send(blocks[3], -1)
-        return add(blocks[0], behind, send(add(blocks[1], send(blocks[2], 1)), 1))
-
-    def ring_scatter(send, blocks):
-        cut = blocks[0].shape[0] // 2
-        low, high = [b[:cut] for b in blocks], [b[cut:] for b in blocks]
-        far_low, far_high = send(low[2], 1), send(high[2], -1)
-        got_high, got_low = send(high[1], 1), send(low[3], -1)
-        sums = lax.optimization_barrier((add(low[1], far_low), add(high[3], far_high)))
+    def ring_scatter(send, own, ahead, behind, far):
+        cut = own.shape[0] // 2
+        far_low, far_high = send(far[:cut], 1), send(far[cut:], -1)
+        got_high, got_low = send(ahead[cut:], 1), send(behind[:cut], -1)
+        sums = lax.optimization_barrier((add(ahead[:cut], far_low), add(behind[cut:], far_high)))
         last_low, last_high = send(sums[0], 1), send(sums[1], -1)
-        return add(low[0], got_low, last_low), add(high[0], got_high, last_high)
+        return add(own[:cut], got_low, last_low), add(own[cut:], got_high, last_high)
 
     lanes = jnp.arange(lane, dtype=jnp.int32)
     hits = routes[:, :, None] == lanes[None, None, :]
@@ -87,8 +78,8 @@
     line = line.reshape(members * rows, half + lane)
     line_rows = members * rows
 
-    plane = small_gather(inner, line)
-    low, high = [jnp.concatenate(plane[k : k + 2], axis=0) for k in (0, 2)]
+    plane, _ = ring_gather(inner, *jnp.split(line, 2))
+    low, high = jnp.concatenate(plane[:4], axis=0), jnp.concatenate(plane[4:], axis=0)
     low, high, w_gate, w_up, w_down = lax.optimization_barrier(
         (low, high, w_gate, w_up, w_down)
     )
@@ -113,10 +104,14 @@
 
     blocks, (w_own, down_own, down_got) = ring_gather(outer, low, high, (w_own, down_own, down_got))
     w_out = jnp.concatenate([down_own, down_got], axis=0)
-    everyone = jnp.concatenate(blocks, axis=0)
+    row_parts = [jnp.concatenate(b, axis=0) for b in (blocks[:6], blocks[6:])]
 
     def project(w):
-        return jnp.dot(everyone[:, :half], w, preferred_element_type=jnp.float32)
+        def dot(part):
+            return jnp.dot(part[:, :half], w, preferred_element_type=jnp.float32)
+
+        near = dot(row_parts[0])
+        return near, dot(row_parts[1])
 
     def swapped(v):
         v = v.reshape(ring, ring, line_rows, v.shape[1])
@@ -127,9 +122,14 @@
     quant_gain = jnp.repeat(quant_limit / past_amax, hidden_units)
     dequant = jnp.repeat(past_amax / quant_limit, hidden_units)
 
-    got = swapped(pair(project(w_other)))
-    weight = jnp.dot(everyone[:, half:], spread, preferred_element_type=jnp.float32)
-    both_proj = lax.optimization_barrier(project(w_own)) + got
+    got = [pair(part) for part in project(w_other)]
+    own = [lax.optimization_barrier(part) for part in project(w_own)]
+    weight = jnp.dot(
+        jnp.concatenate([part[:, half:] for part in row_parts], axis=0),
+        spread,
+        preferred_element_type=jnp.float32,
+    )
+    both_proj = jnp.concatenate(own, axis=0) + swapped(jnp.concatenate(got, axis=0))
     gate_proj = both_proj[:, :fan]
     up_proj = both_proj[:, fan:]
     hidden = jax.nn.silu(gate_proj) * up_proj
@@ -140,8 +140,9 @@
     both = jnp.concatenate([scaled, swapped(pair(scaled))], axis=1)
     down = jnp.dot(both, w_out, preferred_element_type=jnp.float32).astype(jnp.bfloat16)
 
-    low, high = ring_scatter(outer, jnp.split(down, ring))
-    line_sum = small_scatter(inner, [*jnp.split(low, 2), *jnp.split(high, 2)])
+    low, high = ring_scatter(outer, *jnp.split(down, ring))
+    line_sum = ring_scatter(inner, *jnp.split(low, 2), *jnp.split(high, 2))
+    line_sum = jnp.concatenate(line_sum, axis=0)
 
     def split(v):
         top = lax.reduce_precision(v, 8, 7)

time: 190 us -> 180 us (0.947)
  blocking collectives: 42.8 us -> 18.9 us
  starting transfers between devices: 21.8 us -> 42.7 us
  matrix products: 18.7 us -> 13 us
    all_to_all x1 -> x0, blocking collectives: 23.4 us -> none  [per_device(): lax.all_to_all(outgoing, 'edata', split_axis=0, concat_axis=0, tiled=True)]
    all_to_all x0 -> x1, waiting for transfers between devices: none -> 14.4 us  [per_device(): lax.all_to_all(outgoing, 'edata', split_axis=0, concat_axis=0, tiled=True)]
    ppermute x18 -> x24, waiting for transfers between devices: 87.9 us -> 73.6 us  [shift(): return lax.ppermute(v, ('expert', 'edata'), moves)]
    ppermute x18 -> x24, starting transfers between devices: 21.2 us -> 31.5 us  [shift(): return lax.ppermute(v, ('expert', 'edata'), moves)]
    all_to_all x0 -> x1, starting transfers between devices: none -> 8.57 us  [per_device(): lax.all_to_all(outgoing, 'edata', split_axis=0, concat_axis=0, tiled=True)]
    dot_general x3 -> x5, matrix products: 14.5 us -> 8.85 us  [the longest x4 8.18 us: dot(): return jnp.dot(part[:, :half], w, preferred_element_type=jnp.float32)]
    ppermute x4 -> x5, starting transfers between devices: 0.67 us -> 2.7 us  [pair(): return lax.ppermute(v, 'edata', swap)]
  transfers between devices with their start and end apart: 22 -> 30, of which waited for: 14 -> 19; matrix products, arithmetic and copies ran while one was open for 7% -> 5% of each run, Pallas kernels for 0% -> 0%
where the time goes in v1:
time: 180 us; the launch traced here: 177 us
  waiting for transfers between devices  89.9 us (50%)
  starting transfers between devices  42.7 us (24%)
  blocking collectives  18.9 us (10%)
  matrix products  13 us (7%)
  other arithmetic  7.17 us (4%)
  local copies, waits for them, and re-layouts  4.45 us (2%)
    ppermute x24, waiting for transfers between devices, shift(): return lax.ppermute(v, ('expert', 'edata'), moves)  73.6 us
    ppermute x24, starting transfers between devices, shift(): return lax.ppermute(v, ('expert', 'edata'), moves)  31.5 us
    all_to_all x1, blocking collectives, per_device(): lax.all_to_all(message, 'edata', split_axis=0, concat_axis=0, tiled=True)  18.9 us
    all_to_all x1, waiting for transfers between devices, per_device(): lax.all_to_all(outgoing, 'edata', split_axis=0, concat_axis=0, tiled=True)  14.4 us
    all_to_all x1, starting transfers between devices, per_device(): lax.all_to_all(outgoing, 'edata', split_axis=0, concat_axis=0, tiled=True)  8.57 us
    dot_general x4, matrix products, dot(): return jnp.dot(part[:, :half], w, preferred_element_type=jnp.float32)  8.18 us
    dot_general x1, matrix products, per_device(): jnp.dot(both, w_out, preferred_element_type=jnp.float32)  4.19 us
  transfers between devices with their start and end apart: 30, of which 19 were waited for; matrix products, arithmetic and copies ran while one was open for 5% of the time, Pallas kernels for 0%

profile of v1, /device:TPU:2, one launch (start us, length us, event | category | flops | bytes accessed | tf_op | source)
XLA Modules:
  0.0 177.3 jit_solution(225509782193692918)
XLA Ops:
  0.6 0.8 fusion.29
  1.4 0.7 convert_element_type.112
  2.1 0.8 select_reduce_fusion.1
  3.0 0.9 broadcast_in_dim.24
  3.9 8.6 %all-to-all-start = ((bf16[16,4,3712]{2,1,0:T(4,128)(2,1)}), bf16[16,4,3712]{2,1,0:T(4,128)(2,1)S(1)}, u32[]{:S(2)}, u32[]{:S(2)}) async-start(bf16[16,4,3712]{2,1,0:T(4,128)(2,1)} %bitcast.2), calls=%async_computation | async-start | bytes 950272 | tf_op jit(solution)/shard_map/all_to_all | solution.py:77
  12.4 0.7 broadcast_divide_fusion
  13.1 14.4 %all-to-all-done = bf16[16,4,3712]{2,1,0:T(4,128)(2,1)S(1)} async-done(((bf16[16,4,3712]{2,1,0:T(4,128)(2,1)}), bf16[16,4,3712]{2,1,0:T(4,128)(2,1)S(1)}, u32[]{:S(2)}, u32[]{:S(2)}) %all-to-all-start) | async-done | bytes 475168 | tf_op jit(solution)/shard_map/all_to_all | solution.py:77
  27.7 1.7 collective-permute-start.1
  29.4 1.7 collective-permute-start
  31.1 1.9 %collective-permute-start.2 = (bf16[32,3712]{1,0:T(8,128)(2,1)S(1)}, bf16[32,3712]{1,0:T(8,128)(2,1)S(1)}, u32[]{:S(2)}, u32[]{:S(2)}) collective-permute-start(bf16[32,3712]{1,0:T(8,128)(2,1)S(1)} %split.21), channel_id=1, source_target_pairs={{0,48},{1,193},{2,50},{3,195},{4,52},{5,197},{6,54},{7,199},{8,56}... | collective-permute-start | bytes 712712 | tf_op jit(solution)/shard_map/ppermute | solution.py:35
  33.3 1.8 %collective-permute-done.1 = bf16[32,3712]{1,0:T(8,128)(2,1)S(1)} collective-permute-done((bf16[32,3712]{1,0:T(8,128)(2,1)S(1)}, bf16[32,3712]{1,0:T(8,128)(2,1)S(1)}, u32[]{:S(2)}, u32[]{:S(2)}) %collective-permute-start.1) | collective-permute-done | bytes 237600 | tf_op jit(solution)/shard_map/ppermute | solution.py:35
  35.1 2.9 %collective-permute-done.2 = bf16[32,3712]{1,0:T(8,128)(2,1)S(1)} collective-permute-done((bf16[32,3712]{1,0:T(8,128)(2,1)S(1)}, bf16[32,3712]{1,0:T(8,128)(2,1)S(1)}, u32[]{:S(2)}, u32[]{:S(2)}) %collective-permute-start.2) | collective-permute-done | bytes 237600 | tf_op jit(solution)/shard_map/ppermute | solution.py:35
  38.0 1.6 collective-permute-start.4
  39.6 1.7 collective-permute-start.5
  41.4 4.0 %collective-permute-done.4 = bf16[32,3712]{1,0:T(8,128)(2,1)S(1)} collective-permute-done((bf16[32,3712]{1,0:T(8,128)(2,1)S(1)}, bf16[32,3712]{1,0:T(8,128)(2,1)S(1)}, u32[]{:S(2)}, u32[]{:S(2)}) %collective-permute-start.4) | collective-permute-done | bytes 237600 | tf_op jit(solution)/shard_map/ppermute | solution.py:35
  46.4 1.5 collective-permute-start.7
  48.3 1.3 collective-permute-start.8
  50.6 1.8 %collective-permute-start.13 = (bf16[3584,512]{1,0:T(8,128)(2,1)S(1)}, bf16[3584,512]{1,0:T(8,128)(2,1)S(1)}, u32[]{:S(2)}, u32[]{:S(2)}) collective-permute-start(bf16[3584,512]{1,0:T(8,128)(2,1)S(1)} %pad_maximum_fusion.1), channel_id=1, source_target_pairs={{0,1},{1,0},{2,3},{3,2},{4,5},{5,4},{6,7},{7,6},{8,9},{9,8},{10,11... | collective-permute-start | bytes 11010056 | tf_op jit(solution)/shard_map/ppermute | solution.py:24
  53.0 6.6 %collective-permute-done.6 = bf16[128,3712]{1,0:T(8,128)(2,1)S(1)} collective-permute-done((bf16[128,3712]{1,0:T(8,128)(2,1)S(1)}, bf16[128,3712]{1,0:T(8,128)(2,1)S(1)}, u32[]{:S(2)}, u32[]{:S(2)}) %collective-permute-start.6) | collective-permute-done | bytes 950304 | tf_op jit(solution)/shard_map/ppermute | solution.py:35
  59.7 1.5 collective-permute-start.10
  61.3 8.6 %collective-permute-done.8 = bf16[128,3712]{1,0:T(8,128)(2,1)S(1)} collective-permute-done((bf16[128,3712]{1,0:T(8,128)(2,1)S(1)}, bf16[128,3712]{1,0:T(8,128)(2,1)S(1)}, u32[]{:S(2)}, u32[]{:S(2)}) %collective-permute-start.8) | collective-permute-done | bytes 950304 | tf_op jit(solution)/shard_map/ppermute | solution.py:35
  69.8 1.5 collective-permute-start.11
  72.1 1.3 collective-permute-done.10
  73.5 10.1 %collective-permute-done.11 = bf16[128,3712]{1,0:T(8,128)(2,1)S(1)} collective-permute-done((bf16[128,3712]{1,0:T(8,128)(2,1)S(1)}, bf16[128,3712]{1,0:T(8,128)(2,1)S(1)}, u32[]{:S(2)}, u32[]{:S(2)}) %collective-permute-start.11) | collective-permute-done | bytes 950304 | tf_op jit(solution)/shard_map/ppermute | solution.py:35
  83.7 1.8 %collective-permute-done.12 = bf16[128,3712]{1,0:T(8,128)(2,1)S(1)} collective-permute-done((bf16[128,3712]{1,0:T(8,128)(2,1)S(1)}, bf16[128,3712]{1,0:T(8,128)(2,1)S(1)}, u32[]{:S(2)}, u32[]{:S(2)}) %collective-permute-start.12) | collective-permute-done | bytes 950304 | tf_op jit(solution)/shard_map/ppermute | solution.py:35
  85.6 3.0 %fusion = f32[768,512]{1,0:T(8,128)S(1)} fusion(bf16[3584,512]{1,0:T(8,128)(2,1)S(1)} %collective-permute-done.13, bf16[768,3712]{1,0:T(8,128)(2,1)S(1)} %constant_dynamic-update-slice_fusion), kind=kOutput, calls=%fused_computation.1 | convolution fusion | flops 2818572288 | bytes 10747904 | tf_op jit(solution)/shard_map/dot_general | solution.py:111
  88.7 1.1 fusion.7
  90.4 3.0 %fusion.2 = f32[768,512]{1,0:T(8,128)S(1)} fusion(bf16[3584,512]{1,0:T(8,128)(2,1)S(1)} %pad_maximum_fusion, bf16[768,3712]{1,0:T(8,128)(2,1)S(1)} %constant_dynamic-update-slice_fusion), kind=kOutput, calls=%fused_computation.3 | convolution fusion | flops 2818572288 | bytes 10747904 | tf_op jit(solution)/shard_map/dot_general | solution.py:111
  93.4 1.1 fusion.9
  95.4 0.7 multiply_convert_fusion
  96.2 1.9 %collective-permute-done.16 = bf16[1024,256]{1,0:T(8,128)(2,1)S(1)} collective-permute-done((bf16[1024,256]{1,0:T(8,128)(2,1)S(1)}, bf16[1024,256]{1,0:T(8,128)(2,1)S(1)}, u32[]{:S(2)}, u32[]{:S(2)}) %collective-permute-start.16) | collective-permute-done | bytes 524320 | tf_op jit(solution)/shard_map/ppermute | solution.py:24
  98.1 4.2 %convolution_convert_fusion = bf16[1024,3584]{1,0:T(8,128)(2,1)S(1)} fusion(bf16[256,3584]{1,0:T(8,128)(2,1)S(1)} %collective-permute-done.9, bf16[256,3584]{1,0:T(8,128)(2,1)S(1)} %bitcast.50, bf16[1024,256]{1,0:T(8,128)(2,1)S(1)} %bitcast.52, bf16[1024,256]{1,0:T(8,128)(2,1)S(1)} %get-tuple-element.52), kind=kOutput, calls=%fused_computation | convolution fusion | flops 3771203584 | bytes 12058624 | tf_op jit(solution)/shard_map/dot_general | solution.py:141
  102.6 2.1 %collective-permute-start.18 = (bf16[128,3584]{1,0:T(8,128)(2,1)S(1)}, bf16[128,3584]{1,0:T(8,128)(2,1)S(1)}, u32[]{:S(2)}, u32[]{:S(2)}) collective-permute-start(bf16[128,3584]{1,0:T(8,128)(2,1)S(1)} %get-tuple-element.39), channel_id=1, source_target_pairs={{0,64},{1,17},{2,66},{3,19},{4,68},{5,21},{6,70},{7,23},{8,72},{9,... | collective-permute-start | bytes 2752520 | tf_op jit(solution)/shard_map/ppermute | solution.py:35
  104.7 1.9 %collective-permute-start.17 = (bf16[128,3584]{1,0:T(8,128)(2,1)S(1)}, bf16[128,3584]{1,0:T(8,128)(2,1)S(1)}, u32[]{:S(2)}, u32[]{:S(2)}) collective-permute-start(bf16[128,3584]{1,0:T(8,128)(2,1)S(1)} %get-tuple-element.36), channel_id=1, source_target_pairs={{0,192},{1,49},{2,194},{3,51},{4,196},{5,53},{6,198},{7,55},{8,200... | collective-permute-start | bytes 2752520 | tf_op jit(solution)/shard_map/ppermute | solution.py:35
  106.7 9.3 %collective-permute-done.18 = bf16[128,3584]{1,0:T(8,128)(2,1)S(1)} collective-permute-done((bf16[128,3584]{1,0:T(8,128)(2,1)S(1)}, bf16[128,3584]{1,0:T(8,128)(2,1)S(1)}, u32[]{:S(2)}, u32[]{:S(2)}) %collective-permute-start.18) | collective-permute-done | bytes 917536 | tf_op jit(solution)/shard_map/ppermute | solution.py:35
  116.1 2.0 %collective-permute-done.19 = bf16[128,3584]{1,0:T(8,128)(2,1)S(1)} collective-permute-done((bf16[128,3584]{1,0:T(8,128)(2,1)S(1)}, bf16[128,3584]{1,0:T(8,128)(2,1)S(1)}, u32[]{:S(2)}, u32[]{:S(2)}) %collective-permute-start.19) | collective-permute-done | bytes 917536 | tf_op jit(solution)/shard_map/ppermute | solution.py:35
  118.6 1.3 collective-permute-start.20
  119.9 0.8 collective-permute-start.22
  120.8 7.2 %collective-permute-done.17 = bf16[128,3584]{1,0:T(8,128)(2,1)S(1)} collective-permute-done((bf16[128,3584]{1,0:T(8,128)(2,1)S(1)}, bf16[128,3584]{1,0:T(8,128)(2,1)S(1)}, u32[]{:S(2)}, u32[]{:S(2)}) %collective-permute-start.17) | collective-permute-done | bytes 917536 | tf_op jit(solution)/shard_map/ppermute | solution.py:35
  127.9 7.8 %collective-permute-done.20 = bf16[128,3584]{1,0:T(8,128)(2,1)S(1)} collective-permute-done((bf16[128,3584]{1,0:T(8,128)(2,1)S(1)}, bf16[128,3584]{1,0:T(8,128)(2,1)S(1)}, u32[]{:S(2)}, u32[]{:S(2)}) %collective-permute-start.20) | collective-permute-done | bytes 917536 | tf_op jit(solution)/shard_map/ppermute | solution.py:35
  135.7 2.0 %collective-permute-done.22 = bf16[128,3584]{1,0:T(8,128)(2,1)S(1)} collective-permute-done((bf16[128,3584]{1,0:T(8,128)(2,1)S(1)}, bf16[128,3584]{1,0:T(8,128)(2,1)S(1)}, u32[]{:S(2)}, u32[]{:S(2)}) %collective-permute-start.22) | collective-permute-done | bytes 917536 | tf_op jit(solution)/shard_map/ppermute | solution.py:35
  137.7 0.7 add_convert_fusion.1
  138.5 3.0 %collective-permute-start.25 = (bf16[32,3584]{1,0:T(8,128)(2,1)S(1)}, bf16[32,3584]{1,0:T(8,128)(2,1)S(1)}, u32[]{:S(2)}, u32[]{:S(2)}) collective-permute-start(bf16[32,3584]{1,0:T(8,128)(2,1)S(1)} %get-tuple-element.57), channel_id=1, source_target_pairs={{0,48},{1,193},{2,50},{3,195},{4,52},{5,197},{6,54},{7,199},{8,56}... | collective-permute-start | bytes 688136 | tf_op jit(solution)/shard_map/ppermute | solution.py:35
  141.4 3.2 %collective-permute-start.23 = (bf16[32,3584]{1,0:T(8,128)(2,1)S(1)}, bf16[32,3584]{1,0:T(8,128)(2,1)S(1)}, u32[]{:S(2)}, u32[]{:S(2)}) collective-permute-start(bf16[32,3584]{1,0:T(8,128)(2,1)S(1)} %get-tuple-element.56), channel_id=1, source_target_pairs={{0,48},{1,193},{2,50},{3,195},{4,52},{5,197},{6,54},{7,199},{8,56}... | collective-permute-start | bytes 688136 | tf_op jit(solution)/shard_map/ppermute | solution.py:35
  145.0 3.6 %collective-permute-done.24 = bf16[32,3584]{1,0:T(8,128)(2,1)S(1)} collective-permute-done((bf16[32,3584]{1,0:T(8,128)(2,1)S(1)}, bf16[32,3584]{1,0:T(8,128)(2,1)S(1)}, u32[]{:S(2)}, u32[]{:S(2)}) %collective-permute-start.24) | collective-permute-done | bytes 229408 | tf_op jit(solution)/shard_map/ppermute | solution.py:35
  148.8 3.2 %collective-permute-start.28 = (bf16[32,3584]{1,0:T(8,128)(2,1)S(1)}, bf16[32,3584]{1,0:T(8,128)(2,1)S(1)}, u32[]{:S(2)}, u32[]{:S(2)}) collective-permute-start(bf16[32,3584]{1,0:T(8,128)(2,1)S(1)} %add_convert_fusion.6), channel_id=1, source_target_pairs={{0,48},{1,193},{2,50},{3,195},{4,52},{5,197},{6,54},{7,199},{8,56}... | collective-permute-start | bytes 688136 | tf_op jit(solution)/shard_map/ppermute | solution.py:35
  152.1 4.0 %collective-permute-done.26 = bf16[32,3584]{1,0:T(8,128)(2,1)S(1)} collective-permute-done((bf16[32,3584]{1,0:T(8,128)(2,1)S(1)}, bf16[32,3584]{1,0:T(8,128)(2,1)S(1)}, u32[]{:S(2)}, u32[]{:S(2)}) %collective-permute-start.26) | collective-permute-done | bytes 229408 | tf_op jit(solution)/shard_map/ppermute | solution.py:35
  156.6 18.9 %all_to_all.10 = bf16[16,4,3712]{2,1,0:T(4,128)(2,1)S(1)} all-to-all(bf16[16,4,3712]{2,1,0:T(4,128)(2,1)S(1)} %pad_maximum_fusion.5), channel_id=1, replica_groups=mesh['expert'=16,'edata'=16] {'edata'}, dimensions={0} | all-to-all | bytes 950272 | tf_op jit(solution)/shard_map/all_to_all | solution.py:159
  (77 shorter events, 10.3 us)
Async XLA Ops:
  3.9 23.6 %all-to-all-start = ((bf16[16,4,3712]{2,1,0:T(4,128)(2,1)}), bf16[16,4,3712]{2,1,0:T(4,128)(2,1)S(1)}, u32[]{:S(2)}, u32[]{:S(2)}) async-start(bf16[16,4,3712]{2,1,0:T(4,128)(2,1)} %bitcast.2), calls=%async_computation | async-start | bytes 950272 | tf_op jit(solution)/shard_map/all_to_all | solution.py:77
  27.7 7.4 %collective-permute-start.1 = (bf16[32,3712]{1,0:T(8,128)(2,1)S(1)}, bf16[32,3712]{1,0:T(8,128)(2,1)S(1)}, u32[]{:S(2)}, u32[]{:S(2)}) collective-permute-start(bf16[32,3712]{1,0:T(8,128)(2,1)S(1)} %split.9), channel_id=1, source_target_pairs={{0,16},{1,65},{2,18},{3,67},{4,20},{5,69},{6,22},{7,71},{8,24},{9,... | collective-permute-start | bytes 712712 | tf_op jit(solution)/shard_map/ppermute | solution.py:35
  29.4 11.9 %collective-permute-start = (bf16[32,3712]{1,0:T(8,128)(2,1)S(1)}, bf16[32,3712]{1,0:T(8,128)(2,1)S(1)}, u32[]{:S(2)}, u32[]{:S(2)}) collective-permute-start(bf16[32,3712]{1,0:T(8,128)(2,1)S(1)} %split.9), channel_id=1, source_target_pairs={{0,48},{1,193},{2,50},{3,195},{4,52},{5,197},{6,54},{7,199},{8,56}... | collective-permute-start | bytes 712712 | tf_op jit(solution)/shard_map/ppermute | solution.py:35
  31.1 6.9 %collective-permute-start.2 = (bf16[32,3712]{1,0:T(8,128)(2,1)S(1)}, bf16[32,3712]{1,0:T(8,128)(2,1)S(1)}, u32[]{:S(2)}, u32[]{:S(2)}) collective-permute-start(bf16[32,3712]{1,0:T(8,128)(2,1)S(1)} %split.21), channel_id=1, source_target_pairs={{0,48},{1,193},{2,50},{3,195},{4,52},{5,197},{6,54},{7,199},{8,56}... | collective-permute-start | bytes 712712 | tf_op jit(solution)/shard_map/ppermute | solution.py:35
  33.0 14.9 %copy-start = (bf16[2,128,7168]{2,1,0:T(8,128)(2,1)S(1)}, bf16[2,128,7168]{2,1,0:T(8,128)(2,1)}, u32[]{:S(2)}) copy-start(bf16[2,128,7168]{2,1,0:T(8,128)(2,1)} %param.12) | copy-start | bytes 11010052
  33.1 8.3 %collective-permute-start.3 = (bf16[32,3712]{1,0:T(8,128)(2,1)S(1)}, bf16[32,3712]{1,0:T(8,128)(2,1)S(1)}, u32[]{:S(2)}, u32[]{:S(2)}) collective-permute-start(bf16[32,3712]{1,0:T(8,128)(2,1)S(1)} %split.21), channel_id=1, source_target_pairs={{0,16},{1,65},{2,18},{3,67},{4,20},{5,69},{6,22},{7,71},{8,24},{9,... | collective-permute-start | bytes 712712 | tf_op jit(solution)/shard_map/ppermute | solution.py:35
  38.0 7.3 %collective-permute-start.4 = (bf16[32,3712]{1,0:T(8,128)(2,1)S(1)}, bf16[32,3712]{1,0:T(8,128)(2,1)S(1)}, u32[]{:S(2)}, u32[]{:S(2)}) collective-permute-start(bf16[32,3712]{1,0:T(8,128)(2,1)S(1)} %collective-permute-done.1), channel_id=1, source_target_pairs={{0,16},{1,65},{2,18},{3,67},{4,20},{5,69},{6,22},{7,71},{8,24},{9,... | collective-permute-start | bytes 712712 | tf_op jit(solution)/shard_map/ppermute | solution.py:35
  39.6 6.1 %collective-permute-start.5 = (bf16[32,3712]{1,0:T(8,128)(2,1)S(1)}, bf16[32,3712]{1,0:T(8,128)(2,1)S(1)}, u32[]{:S(2)}, u32[]{:S(2)}) collective-permute-start(bf16[32,3712]{1,0:T(8,128)(2,1)S(1)} %collective-permute-done.2), channel_id=1, source_target_pairs={{0,48},{1,193},{2,50},{3,195},{4,52},{5,197},{6,54},{7,199},{8,56}... | collective-permute-start | bytes 712712 | tf_op jit(solution)/shard_map/ppermute | solution.py:35
  45.8 3.8 %copy-start.1 = (bf16[2,7168,128]{2,1,0:T(8,128)(2,1)S(1)}, bf16[2,7168,128]{2,1,0:T(8,128)(2,1)}, u32[]{:S(2)}) copy-start(bf16[2,7168,128]{2,1,0:T(8,128)(2,1)} %param.11) | copy-start | bytes 11010052
  45.8 3.8 %copy-start.2 = (bf16[2,7168,128]{2,1,0:T(8,128)(2,1)S(1)}, bf16[2,7168,128]{2,1,0:T(8,128)(2,1)}, u32[]{:S(2)}) copy-start(bf16[2,7168,128]{2,1,0:T(8,128)(2,1)} %param.10) | copy-start | bytes 11010052
  45.8 13.8 %collective-permute-start.6 = (bf16[128,3712]{1,0:T(8,128)(2,1)S(1)}, bf16[128,3712]{1,0:T(8,128)(2,1)S(1)}, u32[]{:S(2)}, u32[]{:S(2)}) collective-permute-start(bf16[128,3712]{1,0:T(8,128)(2,1)S(1)} %pad_maximum_fusion.3), channel_id=1, source_target_pairs={{0,192},{1,49},{2,194},{3,51},{4,196},{5,53},{6,198},{7,55},{8,200... | collective-permute-start | bytes 2850824 | tf_op jit(solution)/shard_map/ppermute | solution.py:35
  46.4 14.8 %collective-permute-start.7 = (bf16[128,3712]{1,0:T(8,128)(2,1)S(1)}, bf16[128,3712]{1,0:T(8,128)(2,1)S(1)}, u32[]{:S(2)}, u32[]{:S(2)}) collective-permute-start(bf16[128,3712]{1,0:T(8,128)(2,1)S(1)} %pad_maximum_fusion.3), channel_id=1, source_target_pairs={{0,64},{1,17},{2,66},{3,19},{4,68},{5,21},{6,70},{7,23},{8,72},{9,... | collective-permute-start | bytes 2850824 | tf_op jit(solution)/shard_map/ppermute | solution.py:35
  48.2 21.7 %collective-permute-start.9 = (bf16[256,3584]{1,0:T(8,128)(2,1)S(1)}, bf16[256,3584]{1,0:T(8,128)(2,1)S(1)}, u32[]{:S(2)}, u32[]{:S(2)}) collective-permute-start(bf16[256,3584]{1,0:T(8,128)(2,1)S(1)} %bitcast.51), channel_id=1, source_target_pairs={{0,1},{1,0},{2,3},{3,2},{4,5},{5,4},{6,7},{7,6},{8,9},{9,8},{10,11... | collective-permute-start | bytes 5505032 | tf_op jit(solution)/shard_map/ppermute | solution.py:24
  48.3 21.6 %collective-permute-start.8 = (bf16[128,3712]{1,0:T(8,128)(2,1)S(1)}, bf16[128,3712]{1,0:T(8,128)(2,1)S(1)}, u32[]{:S(2)}, u32[]{:S(2)}) collective-permute-start(bf16[128,3712]{1,0:T(8,128)(2,1)S(1)} %pad_maximum_fusion.4), channel_id=1, source_target_pairs={{0,192},{1,49},{2,194},{3,51},{4,196},{5,53},{6,198},{7,55},{8,200... | collective-permute-start | bytes 2850824 | tf_op jit(solution)/shard_map/ppermute | solution.py:35
  50.6 35.0 %collective-permute-start.13 = (bf16[3584,512]{1,0:T(8,128)(2,1)S(1)}, bf16[3584,512]{1,0:T(8,128)(2,1)S(1)}, u32[]{:S(2)}, u32[]{:S(2)}) collective-permute-start(bf16[3584,512]{1,0:T(8,128)(2,1)S(1)} %pad_maximum_fusion.1), channel_id=1, source_target_pairs={{0,1},{1,0},{2,3},{3,2},{4,5},{5,4},{6,7},{7,6},{8,9},{9,8},{10,11... | collective-permute-start | bytes 11010056 | tf_op jit(solution)/shard_map/ppermute | solution.py:24
  59.7 13.7 %collective-permute-start.10 = (bf16[128,3712]{1,0:T(8,128)(2,1)S(1)}, bf16[128,3712]{1,0:T(8,128)(2,1)S(1)}, u32[]{:S(2)}, u32[]{:S(2)}) collective-permute-start(bf16[128,3712]{1,0:T(8,128)(2,1)S(1)} %pad_maximum_fusion.4), channel_id=1, source_target_pairs={{0,64},{1,17},{2,66},{3,19},{4,68},{5,21},{6,70},{7,23},{8,72},{9,... | collective-permute-start | bytes 2850824 | tf_op jit(solution)/shard_map/ppermute | solution.py:35
  69.8 13.7 %collective-permute-start.11 = (bf16[128,3712]{1,0:T(8,128)(2,1)S(1)}, bf16[128,3712]{1,0:T(8,128)(2,1)S(1)}, u32[]{:S(2)}, u32[]{:S(2)}) collective-permute-start(bf16[128,3712]{1,0:T(8,128)(2,1)S(1)} %collective-permute-done.7), channel_id=1, source_target_pairs={{0,64},{1,17},{2,66},{3,19},{4,68},{5,21},{6,70},{7,23},{8,72},{9,... | collective-permute-start | bytes 2850824 | tf_op jit(solution)/shard_map/ppermute | solution.py:35
  71.3 14.1 %collective-permute-start.12 = (bf16[128,3712]{1,0:T(8,128)(2,1)S(1)}, bf16[128,3712]{1,0:T(8,128)(2,1)S(1)}, u32[]{:S(2)}, u32[]{:S(2)}) collective-permute-start(bf16[128,3712]{1,0:T(8,128)(2,1)S(1)} %collective-permute-done.8), channel_id=1, source_target_pairs={{0,192},{1,49},{2,194},{3,51},{4,196},{5,53},{6,198},{7,55},{8,200... | collective-permute-start | bytes 2850824 | tf_op jit(solution)/shard_map/ppermute | solution.py:35
  88.6 5.9 %collective-permute-start.14 = (f32[768,512]{1,0:T(8,128)S(1)}, f32[768,512]{1,0:T(8,128)S(1)}, u32[]{:S(2)}, u32[]{:S(2)}) collective-permute-start(f32[768,512]{1,0:T(8,128)S(1)} %fusion), channel_id=1, source_target_pairs={{0,1},{1,0},{2,3},{3,2},{4,5},{5,4},{6,7},{7,6},{8,9},{9,8},{10,11... | collective-permute-start | bytes 4718600 | tf_op jit(solution)/shard_map/ppermute | solution.py:24
  89.8 4.7 %collective-permute-start.15 = (f32[256,512]{1,0:T(8,128)S(1)}, f32[256,512]{1,0:T(8,128)S(1)}, u32[]{:S(2)}, u32[]{:S(2)}) collective-permute-start(f32[256,512]{1,0:T(8,128)S(1)} %fusion.7), channel_id=1, source_target_pairs={{0,1},{1,0},{2,3},{3,2},{4,5},{5,4},{6,7},{7,6},{8,9},{9,8},{10,11... | collective-permute-start | bytes 1572872 | tf_op jit(solution)/shard_map/ppermute | solution.py:24
  96.1 2.0 %collective-permute-start.16 = (bf16[1024,256]{1,0:T(8,128)(2,1)S(1)}, bf16[1024,256]{1,0:T(8,128)(2,1)S(1)}, u32[]{:S(2)}, u32[]{:S(2)}) collective-permute-start(bf16[1024,256]{1,0:T(8,128)(2,1)S(1)} %get-tuple-element.52), channel_id=1, source_target_pairs={{0,1},{1,0},{2,3},{3,2},{4,5},{5,4},{6,7},{7,6},{8,9},{9,8},{10,11... | collective-permute-start | bytes 1572872 | tf_op jit(solution)/shard_map/ppermute | solution.py:24
  102.6 13.5 %collective-permute-start.18 = (bf16[128,3584]{1,0:T(8,128)(2,1)S(1)}, bf16[128,3584]{1,0:T(8,128)(2,1)S(1)}, u32[]{:S(2)}, u32[]{:S(2)}) collective-permute-start(bf16[128,3584]{1,0:T(8,128)(2,1)S(1)} %get-tuple-element.39), channel_id=1, source_target_pairs={{0,64},{1,17},{2,66},{3,19},{4,68},{5,21},{6,70},{7,23},{8,72},{9,... | collective-permute-start | bytes 2752520 | tf_op jit(solution)/shard_map/ppermute | solution.py:35
  104.7 13.4 %collective-permute-start.19 = (bf16[128,3584]{1,0:T(8,128)(2,1)S(1)}, bf16[128,3584]{1,0:T(8,128)(2,1)S(1)}, u32[]{:S(2)}, u32[]{:S(2)}) collective-permute-start(bf16[128,3584]{1,0:T(8,128)(2,1)S(1)} %get-tuple-element.38), channel_id=1, source_target_pairs={{0,192},{1,49},{2,194},{3,51},{4,196},{5,53},{6,198},{7,55},{8,200... | collective-permute-start | bytes 2752520 | tf_op jit(solution)/shard_map/ppermute | solution.py:35
  104.7 23.2 %collective-permute-start.17 = (bf16[128,3584]{1,0:T(8,128)(2,1)S(1)}, bf16[128,3584]{1,0:T(8,128)(2,1)S(1)}, u32[]{:S(2)}, u32[]{:S(2)}) collective-permute-start(bf16[128,3584]{1,0:T(8,128)(2,1)S(1)} %get-tuple-element.36), channel_id=1, source_target_pairs={{0,192},{1,49},{2,194},{3,51},{4,196},{5,53},{6,198},{7,55},{8,200... | collective-permute-start | bytes 2752520 | tf_op jit(solution)/shard_map/ppermute | solution.py:35
  106.6 21.3 %collective-permute-start.21 = (bf16[128,3584]{1,0:T(8,128)(2,1)S(1)}, bf16[128,3584]{1,0:T(8,128)(2,1)S(1)}, u32[]{:S(2)}, u32[]{:S(2)}) collective-permute-start(bf16[128,3584]{1,0:T(8,128)(2,1)S(1)} %get-tuple-element.37), channel_id=1, source_target_pairs={{0,64},{1,17},{2,66},{3,19},{4,68},{5,21},{6,70},{7,23},{8,72},{9,... | collective-permute-start | bytes 2752520 | tf_op jit(solution)/shard_map/ppermute | solution.py:35
  118.6 17.1 %collective-permute-start.20 = (bf16[128,3584]{1,0:T(8,128)(2,1)S(1)}, bf16[128,3584]{1,0:T(8,128)(2,1)S(1)}, u32[]{:S(2)}, u32[]{:S(2)}) collective-permute-start(bf16[128,3584]{1,0:T(8,128)(2,1)S(1)} %get-tuple-element.30), channel_id=1, source_target_pairs={{0,64},{1,17},{2,66},{3,19},{4,68},{5,21},{6,70},{7,23},{8,72},{9,... | collective-permute-start | bytes 2752520 | tf_op jit(solution)/shard_map/ppermute | solution.py:35
  119.9 17.8 %collective-permute-start.22 = (bf16[128,3584]{1,0:T(8,128)(2,1)S(1)}, bf16[128,3584]{1,0:T(8,128)(2,1)S(1)}, u32[]{:S(2)}, u32[]{:S(2)}) collective-permute-start(bf16[128,3584]{1,0:T(8,128)(2,1)S(1)} %get-tuple-element.31), channel_id=1, source_target_pairs={{0,192},{1,49},{2,194},{3,51},{4,196},{5,53},{6,198},{7,55},{8,200... | collective-permute-start | bytes 2752520 | tf_op jit(solution)/shard_map/ppermute | solution.py:35
  138.5 6.5 %collective-permute-start.25 = (bf16[32,3584]{1,0:T(8,128)(2,1)S(1)}, bf16[32,3584]{1,0:T(8,128)(2,1)S(1)}, u32[]{:S(2)}, u32[]{:S(2)}) collective-permute-start(bf16[32,3584]{1,0:T(8,128)(2,1)S(1)} %get-tuple-element.57), channel_id=1, source_target_pairs={{0,48},{1,193},{2,50},{3,195},{4,52},{5,197},{6,54},{7,199},{8,56}... | collective-permute-start | bytes 688136 | tf_op jit(solution)/shard_map/ppermute | solution.py:35
  141.4 7.2 %collective-permute-start.24 = (bf16[32,3584]{1,0:T(8,128)(2,1)S(1)}, bf16[32,3584]{1,0:T(8,128)(2,1)S(1)}, u32[]{:S(2)}, u32[]{:S(2)}) collective-permute-start(bf16[32,3584]{1,0:T(8,128)(2,1)S(1)} %get-tuple-element.58), channel_id=1, source_target_pairs={{0,16},{1,65},{2,18},{3,67},{4,20},{5,69},{6,22},{7,71},{8,24},{9,... | collective-permute-start | bytes 688136 | tf_op jit(solution)/shard_map/ppermute | solution.py:35
  141.4 10.6 %collective-permute-start.23 = (bf16[32,3584]{1,0:T(8,128)(2,1)S(1)}, bf16[32,3584]{1,0:T(8,128)(2,1)S(1)}, u32[]{:S(2)}, u32[]{:S(2)}) collective-permute-start(bf16[32,3584]{1,0:T(8,128)(2,1)S(1)} %get-tuple-element.56), channel_id=1, source_target_pairs={{0,48},{1,193},{2,50},{3,195},{4,52},{5,197},{6,54},{7,199},{8,56}... | collective-permute-start | bytes 688136 | tf_op jit(solution)/shard_map/ppermute | solution.py:35
  144.7 7.4 %collective-permute-start.27 = (bf16[32,3584]{1,0:T(8,128)(2,1)S(1)}, bf16[32,3584]{1,0:T(8,128)(2,1)S(1)}, u32[]{:S(2)}, u32[]{:S(2)}) collective-permute-start(bf16[32,3584]{1,0:T(8,128)(2,1)S(1)} %slice.195), channel_id=1, source_target_pairs={{0,16},{1,65},{2,18},{3,67},{4,20},{5,69},{6,22},{7,71},{8,24},{9,... | collective-permute-start | bytes 688136 | tf_op jit(solution)/shard_map/ppermute | solution.py:35
  148.7 7.3 %collective-permute-start.26 = (bf16[32,3584]{1,0:T(8,128)(2,1)S(1)}, bf16[32,3584]{1,0:T(8,128)(2,1)S(1)}, u32[]{:S(2)}, u32[]{:S(2)}) collective-permute-start(bf16[32,3584]{1,0:T(8,128)(2,1)S(1)} %add_convert_fusion.7), channel_id=1, source_target_pairs={{0,16},{1,65},{2,18},{3,67},{4,20},{5,69},{6,22},{7,71},{8,24},{9,... | collective-permute-start | bytes 688136 | tf_op jit(solution)/shard_map/ppermute | solution.py:35
  148.8 7.2 %collective-permute-start.28 = (bf16[32,3584]{1,0:T(8,128)(2,1)S(1)}, bf16[32,3584]{1,0:T(8,128)(2,1)S(1)}, u32[]{:S(2)}, u32[]{:S(2)}) collective-permute-start(bf16[32,3584]{1,0:T(8,128)(2,1)S(1)} %add_convert_fusion.6), channel_id=1, source_target_pairs={{0,48},{1,193},{2,50},{3,195},{4,52},{5,197},{6,54},{7,199},{8,56}... | collective-permute-start | bytes 688136 | tf_op jit(solution)/shard_map/ppermute | solution.py:35

commit v2 on v1

--- a/solution.py
+++ b/solution.py
@@ -47,8 +47,8 @@
             (behind_low, ahead_high, ready)
         )
         far = [send(behind_low, 1), send(ahead_high, -1)]
-        halves = [low, high, ahead_low, ahead_high, behind_low, behind_high, *far]
-        return halves, ready
+        near = [low, high, ahead_low, ahead_high, behind_low, behind_high]
+        return [*lax.optimization_barrier(near), *far], ready
 
     def add(*parts):
         return sum(p.astype(jnp.float32) for p in parts).astype(jnp.bfloat16)
@@ -138,9 +138,15 @@
     clipped = jnp.clip(hidden * quant_gain[None, :], -quant_limit, quant_limit)
     scaled = (clipped * (weight * dequant[None, :])).astype(jnp.bfloat16)
     both = jnp.concatenate([scaled, swapped(pair(scaled))], axis=1)
-    down = jnp.dot(both, w_out, preferred_element_type=jnp.float32).astype(jnp.bfloat16)
+    cut = both.shape[0] // ring * (ring - 1)
 
-    low, high = ring_scatter(outer, *jnp.split(down, ring))
+    def down(part):
+        return jnp.dot(part, w_out, preferred_element_type=jnp.float32).astype(jnp.bfloat16)
+
+    rest = down(both[:cut])
+    down_blocks = [*jnp.split(rest, ring - 1), down(both[cut:])]
+
+    low, high = ring_scatter(outer, *down_blocks)
     line_sum = ring_scatter(inner, *jnp.split(low, 2), *jnp.split(high, 2))
     line_sum = jnp.concatenate(line_sum, axis=0)
 

time: 180 us -> 182 us (1.011)
  blocking collectives: 18.9 us -> 42.4 us
  waiting for transfers between devices: 89.9 us -> 76.9 us
  starting transfers between devices: 42.7 us -> 34.1 us
    all_to_all x0 -> x1, blocking collectives: none -> 23.4 us  [per_device(): lax.all_to_all(outgoing, 'edata', split_axis=0, concat_axis=0, tiled=True)]
    all_to_all x1 -> x0, waiting for transfers between devices: 14.4 us -> none  [per_device(): lax.all_to_all(outgoing, 'edata', split_axis=0, concat_axis=0, tiled=True)]
    all_to_all x1 -> x0, starting transfers between devices: 8.57 us -> none  [per_device(): lax.all_to_all(outgoing, 'edata', split_axis=0, concat_axis=0, tiled=True)]
    dot_general x1 -> x2, matrix products: 4.19 us -> 4.35 us  [down(): jnp.dot(part, w_out, preferred_element_type=jnp.float32)]
  transfers between devices with their start and end apart: 30 -> 29, of which waited for: 19 -> 16; matrix products, arithmetic and copies ran while one was open for 5% -> 5% of each run, Pallas kernels for 0% -> 0%
where the time goes in v2:
time: 182 us; the launch traced here: 179 us
  waiting for transfers between devices  76.9 us (42%)
  blocking collectives  42.4 us (23%)
  starting transfers between devices  34.1 us (19%)
  matrix products  13.2 us (7%)
  other arithmetic  6.4 us (4%)
  local copies, waits for them, and re-layouts  5.13 us (3%)
    ppermute x24, waiting for transfers between devices, shift(): return lax.ppermute(v, ('expert', 'edata'), moves)  75.3 us
    ppermute x24, starting transfers between devices, shift(): return lax.ppermute(v, ('expert', 'edata'), moves)  31.4 us
    all_to_all x1, blocking collectives, per_device(): lax.all_to_all(outgoing, 'edata', split_axis=0, concat_axis=0, tiled=True)  23.4 us
    all_to_all x1, blocking collectives, per_device(): lax.all_to_all(message, 'edata', split_axis=0, concat_axis=0, tiled=True)  18.9 us
    dot_general x4, matrix products, dot(): return jnp.dot(part[:, :half], w, preferred_element_type=jnp.float32)  8.18 us
    dot_general x2, matrix products, down(): jnp.dot(part, w_out, preferred_element_type=jnp.float32)  4.35 us
  transfers between devices with their start and end apart: 29, of which 16 were waited for; matrix products, arithmetic and copies ran while one was open for 5% of the time, Pallas kernels for 0%

profile of v2, /device:TPU:2, one launch (start us, length us, event | category | flops | bytes accessed | tf_op | source)
XLA Modules:
  0.0 179.2 jit_solution(10250253442648771497)
XLA Ops:
  0.6 0.8 fusion.28
  1.4 0.7 convert_element_type.115
  2.1 0.8 select_reduce_fusion.1
  3.1 23.4 %all_to_all.10 = bf16[16,4,3712]{2,1,0:T(4,128)(2,1)S(1)} all-to-all(bf16[16,4,3712]{2,1,0:T(4,128)(2,1)S(1)} %bitcast.54), channel_id=1, replica_groups=mesh['expert'=16,'edata'=16] {'edata'}, dimensions={0} | all-to-all | bytes 950272 | tf_op jit(solution)/shard_map/all_to_all | solution.py:77
  26.8 1.7 collective-permute-start.1
  28.4 1.7 collective-permute-start
  30.2 1.9 %collective-permute-start.2 = (bf16[32,3712]{1,0:T(8,128)(2,1)S(1)}, bf16[32,3712]{1,0:T(8,128)(2,1)S(1)}, u32[]{:S(2)}, u32[]{:S(2)}) collective-permute-start(bf16[32,3712]{1,0:T(8,128)(2,1)S(1)} %split.20), channel_id=1, source_target_pairs={{0,48},{1,193},{2,50},{3,195},{4,52},{5,197},{6,54},{7,199},{8,56}... | collective-permute-start | bytes 712712 | tf_op jit(solution)/shard_map/ppermute | solution.py:35
  32.3 1.8 %collective-permute-done.1 = bf16[32,3712]{1,0:T(8,128)(2,1)S(1)} collective-permute-done((bf16[32,3712]{1,0:T(8,128)(2,1)S(1)}, bf16[32,3712]{1,0:T(8,128)(2,1)S(1)}, u32[]{:S(2)}, u32[]{:S(2)}) %collective-permute-start.1) | collective-permute-done | bytes 237600 | tf_op jit(solution)/shard_map/ppermute | solution.py:35
  34.2 2.9 %collective-permute-done.2 = bf16[32,3712]{1,0:T(8,128)(2,1)S(1)} collective-permute-done((bf16[32,3712]{1,0:T(8,128)(2,1)S(1)}, bf16[32,3712]{1,0:T(8,128)(2,1)S(1)}, u32[]{:S(2)}, u32[]{:S(2)}) %collective-permute-start.2) | collective-permute-done | bytes 237600 | tf_op jit(solution)/shard_map/ppermute | solution.py:35
  37.1 1.6 collective-permute-start.4
  38.7 1.7 collective-permute-start.5
  40.4 4.0 %collective-permute-done.4 = bf16[32,3712]{1,0:T(8,128)(2,1)S(1)} collective-permute-done((bf16[32,3712]{1,0:T(8,128)(2,1)S(1)}, bf16[32,3712]{1,0:T(8,128)(2,1)S(1)}, u32[]{:S(2)}, u32[]{:S(2)}) %collective-permute-start.4) | collective-permute-done | bytes 237600 | tf_op jit(solution)/shard_map/ppermute | solution.py:35
  45.2 0.6 collective-permute-start.8
  45.9 1.5 collective-permute-start.10
  47.4 1.5 collective-permute-start.7
  50.8 19.8 %collective-permute-done.7 = bf16[128,3712]{1,0:T(8,128)(2,1)S(1)} collective-permute-done((bf16[128,3712]{1,0:T(8,128)(2,1)S(1)}, bf16[128,3712]{1,0:T(8,128)(2,1)S(1)}, u32[]{:S(2)}, u32[]{:S(2)}) %collective-permute-start.7) | collective-permute-done | bytes 950304 | tf_op jit(solution)/shard_map/ppermute | solution.py:35
  70.5 1.8 %collective-permute-start.13 = (bf16[3584,512]{1,0:T(8,128)(2,1)S(1)}, bf16[3584,512]{1,0:T(8,128)(2,1)S(1)}, u32[]{:S(2)}, u32[]{:S(2)}) collective-permute-start(bf16[3584,512]{1,0:T(8,128)(2,1)S(1)} %pad_maximum_fusion.1), channel_id=1, source_target_pairs={{0,1},{1,0},{2,3},{3,2},{4,5},{5,4},{6,7},{7,6},{8,9},{9,8},{10,11... | collective-permute-start | bytes 11010056 | tf_op jit(solution)/shard_map/ppermute | solution.py:24
  72.3 1.5 collective-permute-start.11
  74.6 1.3 constant_dynamic-update-slice_fusion.3
  76.2 9.8 %collective-permute-done.11 = bf16[128,3712]{1,0:T(8,128)(2,1)S(1)} collective-permute-done((bf16[128,3712]{1,0:T(8,128)(2,1)S(1)}, bf16[128,3712]{1,0:T(8,128)(2,1)S(1)}, u32[]{:S(2)}, u32[]{:S(2)}) %collective-permute-start.11) | collective-permute-done | bytes 950304 | tf_op jit(solution)/shard_map/ppermute | solution.py:35
  86.1 1.4 collective-permute-done.12
  87.7 3.0 %fusion = f32[768,512]{1,0:T(8,128)S(1)} fusion(bf16[3584,512]{1,0:T(8,128)(2,1)S(1)} %collective-permute-done.13, bf16[768,3712]{1,0:T(8,128)(2,1)S(1)} %constant_dynamic-update-slice_fusion), kind=kOutput, calls=%fused_computation.2 | convolution fusion | flops 2818572288 | bytes 10747904 | tf_op jit(solution)/shard_map/dot_general | solution.py:111
  90.8 1.1 fusion.4
  91.9 0.6 collective-permute-start.15
  92.5 3.0 %fusion.2 = f32[768,512]{1,0:T(8,128)S(1)} fusion(bf16[3584,512]{1,0:T(8,128)(2,1)S(1)} %pad_maximum_fusion, bf16[768,3712]{1,0:T(8,128)(2,1)S(1)} %constant_dynamic-update-slice_fusion), kind=kOutput, calls=%fused_computation.4 | convolution fusion | flops 2818572288 | bytes 10747904 | tf_op jit(solution)/shard_map/dot_general | solution.py:111
  95.5 1.1 fusion.6
  97.5 0.7 multiply_convert_fusion
  98.5 1.6 collective-permute-done.16
  100.2 3.2 %convolution_convert_fusion = bf16[768,3584]{1,0:T(8,128)(2,1)S(1)} fusion(bf16[512,3584]{1,0:T(8,128)(2,1)S(1)} %constant_dynamic-update-slice_fusion.8, bf16[1024,256]{1,0:T(8,128)(2,1)S(1)} %get-tuple-element.74, bf16[1024,256]{1,0:T(8,128)(2,1)S(1)} %bitcast.52), kind=kOutput, calls=%fused_computation | convolution fusion | flops 2822897664 | bytes 10223616 | tf_op jit(solution)/shard_map/dot_general | solution.py:144
  103.5 1.1 convolution_convert_fusion.1
  104.7 1.3 collective-permute-start.18
  106.0 0.8 collective-permute-start.19
  107.0 2.8 %collective-permute-start.17 = (bf16[128,3584]{1,0:T(8,128)(2,1)S(1)}, bf16[128,3584]{1,0:T(8,128)(2,1)S(1)}, u32[]{:S(2)}, u32[]{:S(2)}) collective-permute-start(bf16[128,3584]{1,0:T(8,128)(2,1)S(1)} %get-tuple-element.60), channel_id=1, source_target_pairs={{0,192},{1,49},{2,194},{3,51},{4,196},{5,53},{6,198},{7,55},{8,200... | collective-permute-start | bytes 2752520 | tf_op jit(solution)/shard_map/ppermute | solution.py:35
  109.8 8.4 %collective-permute-done.18 = bf16[128,3584]{1,0:T(8,128)(2,1)S(1)} collective-permute-done((bf16[128,3584]{1,0:T(8,128)(2,1)S(1)}, bf16[128,3584]{1,0:T(8,128)(2,1)S(1)}, u32[]{:S(2)}, u32[]{:S(2)}) %collective-permute-start.18) | collective-permute-done | bytes 917536 | tf_op jit(solution)/shard_map/ppermute | solution.py:35
  118.2 1.8 %collective-permute-done.19 = bf16[128,3584]{1,0:T(8,128)(2,1)S(1)} collective-permute-done((bf16[128,3584]{1,0:T(8,128)(2,1)S(1)}, bf16[128,3584]{1,0:T(8,128)(2,1)S(1)}, u32[]{:S(2)}, u32[]{:S(2)}) %collective-permute-start.19) | collective-permute-done | bytes 917536 | tf_op jit(solution)/shard_map/ppermute | solution.py:35
  120.5 2.1 %collective-permute-start.20 = (bf16[128,3584]{1,0:T(8,128)(2,1)S(1)}, bf16[128,3584]{1,0:T(8,128)(2,1)S(1)}, u32[]{:S(2)}, u32[]{:S(2)}) collective-permute-start(bf16[128,3584]{1,0:T(8,128)(2,1)S(1)} %get-tuple-element.54), channel_id=1, source_target_pairs={{0,64},{1,17},{2,66},{3,19},{4,68},{5,21},{6,70},{7,23},{8,72},{9,... | collective-permute-start | bytes 2752520 | tf_op jit(solution)/shard_map/ppermute | solution.py:35
  122.6 7.3 %collective-permute-done.17 = bf16[128,3584]{1,0:T(8,128)(2,1)S(1)} collective-permute-done((bf16[128,3584]{1,0:T(8,128)(2,1)S(1)}, bf16[128,3584]{1,0:T(8,128)(2,1)S(1)}, u32[]{:S(2)}, u32[]{:S(2)}) %collective-permute-start.17) | collective-permute-done | bytes 917536 | tf_op jit(solution)/shard_map/ppermute | solution.py:35
  129.9 8.0 %collective-permute-done.20 = bf16[128,3584]{1,0:T(8,128)(2,1)S(1)} collective-permute-done((bf16[128,3584]{1,0:T(8,128)(2,1)S(1)}, bf16[128,3584]{1,0:T(8,128)(2,1)S(1)}, u32[]{:S(2)}, u32[]{:S(2)}) %collective-permute-start.20) | collective-permute-done | bytes 917536 | tf_op jit(solution)/shard_map/ppermute | solution.py:35
  137.9 1.8 %collective-permute-done.22 = bf16[128,3584]{1,0:T(8,128)(2,1)S(1)} collective-permute-done((bf16[128,3584]{1,0:T(8,128)(2,1)S(1)}, bf16[128,3584]{1,0:T(8,128)(2,1)S(1)}, u32[]{:S(2)}, u32[]{:S(2)}) %collective-permute-start.22) | collective-permute-done | bytes 917536 | tf_op jit(solution)/shard_map/ppermute | solution.py:35
  139.7 0.7 add_convert_fusion.1
  140.4 3.0 %collective-permute-start.25 = (bf16[32,3584]{1,0:T(8,128)(2,1)S(1)}, bf16[32,3584]{1,0:T(8,128)(2,1)S(1)}, u32[]{:S(2)}, u32[]{:S(2)}) collective-permute-start(bf16[32,3584]{1,0:T(8,128)(2,1)S(1)} %get-tuple-element.81), channel_id=1, source_target_pairs={{0,48},{1,193},{2,50},{3,195},{4,52},{5,197},{6,54},{7,199},{8,56}... | collective-permute-start | bytes 688136 | tf_op jit(solution)/shard_map/ppermute | solution.py:35
  143.4 3.2 %collective-permute-start.23 = (bf16[32,3584]{1,0:T(8,128)(2,1)S(1)}, bf16[32,3584]{1,0:T(8,128)(2,1)S(1)}, u32[]{:S(2)}, u32[]{:S(2)}) collective-permute-start(bf16[32,3584]{1,0:T(8,128)(2,1)S(1)} %get-tuple-element.80), channel_id=1, source_target_pairs={{0,48},{1,193},{2,50},{3,195},{4,52},{5,197},{6,54},{7,199},{8,56}... | collective-permute-start | bytes 688136 | tf_op jit(solution)/shard_map/ppermute | solution.py:35
  147.0 3.6 %collective-permute-done.24 = bf16[32,3584]{1,0:T(8,128)(2,1)S(1)} collective-permute-done((bf16[32,3584]{1,0:T(8,128)(2,1)S(1)}, bf16[32,3584]{1,0:T(8,128)(2,1)S(1)}, u32[]{:S(2)}, u32[]{:S(2)}) %collective-permute-start.24) | collective-permute-done | bytes 229408 | tf_op jit(solution)/shard_map/ppermute | solution.py:35
  150.8 3.2 %collective-permute-start.28 = (bf16[32,3584]{1,0:T(8,128)(2,1)S(1)}, bf16[32,3584]{1,0:T(8,128)(2,1)S(1)}, u32[]{:S(2)}, u32[]{:S(2)}) collective-permute-start(bf16[32,3584]{1,0:T(8,128)(2,1)S(1)} %add_convert_fusion.6), channel_id=1, source_target_pairs={{0,48},{1,193},{2,50},{3,195},{4,52},{5,197},{6,54},{7,199},{8,56}... | collective-permute-start | bytes 688136 | tf_op jit(solution)/shard_map/ppermute | solution.py:35
  154.0 4.0 %collective-permute-done.26 = bf16[32,3584]{1,0:T(8,128)(2,1)S(1)} collective-permute-done((bf16[32,3584]{1,0:T(8,128)(2,1)S(1)}, bf16[32,3584]{1,0:T(8,128)(2,1)S(1)}, u32[]{:S(2)}, u32[]{:S(2)}) %collective-permute-start.26) | collective-permute-done | bytes 229408 | tf_op jit(solution)/shard_map/ppermute | solution.py:35
  158.6 18.9 %all_to_all.11 = bf16[16,4,3712]{2,1,0:T(4,128)(2,1)S(1)} all-to-all(bf16[16,4,3712]{2,1,0:T(4,128)(2,1)S(1)} %pad_maximum_fusion.5), channel_id=1, replica_groups=mesh['expert'=16,'edata'=16] {'edata'}, dimensions={0} | all-to-all | bytes 950272 | tf_op jit(solution)/shard_map/all_to_all | solution.py:165
  177.9 0.6 fusion.18
  178.6 0.6 pad_maximum_fusion.10
  (82 shorter events, 8.4 us)
Async XLA Ops:
  0.6 31.6 %copy-start.3 = (f32[2]{0:T(128)S(1)}, f32[2]{0:T(128)}, u32[]{:S(2)}) copy-start(f32[2]{0:T(128)} %param.13) | copy-start | bytes 28
  26.8 7.4 %collective-permute-start.1 = (bf16[32,3712]{1,0:T(8,128)(2,1)S(1)}, bf16[32,3712]{1,0:T(8,128)(2,1)S(1)}, u32[]{:S(2)}, u32[]{:S(2)}) collective-permute-start(bf16[32,3712]{1,0:T(8,128)(2,1)S(1)} %split.18), channel_id=1, source_target_pairs={{0,16},{1,65},{2,18},{3,67},{4,20},{5,69},{6,22},{7,71},{8,24},{9,... | collective-permute-start | bytes 712712 | tf_op jit(solution)/shard_map/ppermute | solution.py:35
  28.4 11.9 %collective-permute-start = (bf16[32,3712]{1,0:T(8,128)(2,1)S(1)}, bf16[32,3712]{1,0:T(8,128)(2,1)S(1)}, u32[]{:S(2)}, u32[]{:S(2)}) collective-permute-start(bf16[32,3712]{1,0:T(8,128)(2,1)S(1)} %split.18), channel_id=1, source_target_pairs={{0,48},{1,193},{2,50},{3,195},{4,52},{5,197},{6,54},{7,199},{8,56}... | collective-permute-start | bytes 712712 | tf_op jit(solution)/shard_map/ppermute | solution.py:35
  30.2 6.9 %collective-permute-start.2 = (bf16[32,3712]{1,0:T(8,128)(2,1)S(1)}, bf16[32,3712]{1,0:T(8,128)(2,1)S(1)}, u32[]{:S(2)}, u32[]{:S(2)}) collective-permute-start(bf16[32,3712]{1,0:T(8,128)(2,1)S(1)} %split.20), channel_id=1, source_target_pairs={{0,48},{1,193},{2,50},{3,195},{4,52},{5,197},{6,54},{7,199},{8,56}... | collective-permute-start | bytes 712712 | tf_op jit(solution)/shard_map/ppermute | solution.py:35
  32.0 8.3 %collective-permute-start.3 = (bf16[32,3712]{1,0:T(8,128)(2,1)S(1)}, bf16[32,3712]{1,0:T(8,128)(2,1)S(1)}, u32[]{:S(2)}, u32[]{:S(2)}) collective-permute-start(bf16[32,3712]{1,0:T(8,128)(2,1)S(1)} %split.20), channel_id=1, source_target_pairs={{0,16},{1,65},{2,18},{3,67},{4,20},{5,69},{6,22},{7,71},{8,24},{9,... | collective-permute-start | bytes 712712 | tf_op jit(solution)/shard_map/ppermute | solution.py:35
  32.3 12.6 %copy-start = (bf16[2,128,7168]{2,1,0:T(8,128)(2,1)S(1)}, bf16[2,128,7168]{2,1,0:T(8,128)(2,1)}, u32[]{:S(2)}) copy-start(bf16[2,128,7168]{2,1,0:T(8,128)(2,1)} %param.12) | copy-start | bytes 11010052
  37.1 7.3 %collective-permute-start.4 = (bf16[32,3712]{1,0:T(8,128)(2,1)S(1)}, bf16[32,3712]{1,0:T(8,128)(2,1)S(1)}, u32[]{:S(2)}, u32[]{:S(2)}) collective-permute-start(bf16[32,3712]{1,0:T(8,128)(2,1)S(1)} %collective-permute-done.1), channel_id=1, source_target_pairs={{0,16},{1,65},{2,18},{3,67},{4,20},{5,69},{6,22},{7,71},{8,24},{9,... | collective-permute-start | bytes 712712 | tf_op jit(solution)/shard_map/ppermute | solution.py:35
  38.7 6.1 %collective-permute-start.5 = (bf16[32,3712]{1,0:T(8,128)(2,1)S(1)}, bf16[32,3712]{1,0:T(8,128)(2,1)S(1)}, u32[]{:S(2)}, u32[]{:S(2)}) collective-permute-start(bf16[32,3712]{1,0:T(8,128)(2,1)S(1)} %collective-permute-done.2), channel_id=1, source_target_pairs={{0,48},{1,193},{2,50},{3,195},{4,52},{5,197},{6,54},{7,199},{8,56}... | collective-permute-start | bytes 712712 | tf_op jit(solution)/shard_map/ppermute | solution.py:35
  44.9 4.5 %copy-start.1 = (bf16[2,7168,128]{2,1,0:T(8,128)(2,1)S(1)}, bf16[2,7168,128]{2,1,0:T(8,128)(2,1)}, u32[]{:S(2)}) copy-start(bf16[2,7168,128]{2,1,0:T(8,128)(2,1)} %param.11) | copy-start | bytes 11010052
  44.9 4.5 %copy-start.2 = (bf16[2,7168,128]{2,1,0:T(8,128)(2,1)S(1)}, bf16[2,7168,128]{2,1,0:T(8,128)(2,1)}, u32[]{:S(2)}) copy-start(bf16[2,7168,128]{2,1,0:T(8,128)(2,1)} %param.10) | copy-start | bytes 11010052
  45.1 27.2 %collective-permute-start.9 = (bf16[256,3584]{1,0:T(8,128)(2,1)S(1)}, bf16[256,3584]{1,0:T(8,128)(2,1)S(1)}, u32[]{:S(2)}, u32[]{:S(2)}) collective-permute-start(bf16[256,3584]{1,0:T(8,128)(2,1)S(1)} %bitcast.56), channel_id=1, source_target_pairs={{0,1},{1,0},{2,3},{3,2},{4,5},{5,4},{6,7},{7,6},{8,9},{9,8},{10,11... | collective-permute-start | bytes 5505032 | tf_op jit(solution)/shard_map/ppermute | solution.py:24
  45.2 27.1 %collective-permute-start.8 = (bf16[128,3712]{1,0:T(8,128)(2,1)S(1)}, bf16[128,3712]{1,0:T(8,128)(2,1)S(1)}, u32[]{:S(2)}, u32[]{:S(2)}) collective-permute-start(bf16[128,3712]{1,0:T(8,128)(2,1)S(1)} %pad_maximum_fusion.4), channel_id=1, source_target_pairs={{0,192},{1,49},{2,194},{3,51},{4,196},{5,53},{6,198},{7,55},{8,200... | collective-permute-start | bytes 2850824 | tf_op jit(solution)/shard_map/ppermute | solution.py:35
  45.9 28.5 %collective-permute-start.10 = (bf16[128,3712]{1,0:T(8,128)(2,1)S(1)}, bf16[128,3712]{1,0:T(8,128)(2,1)S(1)}, u32[]{:S(2)}, u32[]{:S(2)}) collective-permute-start(bf16[128,3712]{1,0:T(8,128)(2,1)S(1)} %pad_maximum_fusion.4), channel_id=1, source_target_pairs={{0,64},{1,17},{2,66},{3,19},{4,68},{5,21},{6,70},{7,23},{8,72},{9,... | collective-permute-start | bytes 2850824 | tf_op jit(solution)/shard_map/ppermute | solution.py:35
  47.4 23.2 %collective-permute-start.7 = (bf16[128,3712]{1,0:T(8,128)(2,1)S(1)}, bf16[128,3712]{1,0:T(8,128)(2,1)S(1)}, u32[]{:S(2)}, u32[]{:S(2)}) collective-permute-start(bf16[128,3712]{1,0:T(8,128)(2,1)S(1)} %pad_maximum_fusion.3), channel_id=1, source_target_pairs={{0,64},{1,17},{2,66},{3,19},{4,68},{5,21},{6,70},{7,23},{8,72},{9,... | collective-permute-start | bytes 2850824 | tf_op jit(solution)/shard_map/ppermute | solution.py:35
  48.8 25.5 %collective-permute-start.6 = (bf16[128,3712]{1,0:T(8,128)(2,1)S(1)}, bf16[128,3712]{1,0:T(8,128)(2,1)}, u32[]{:S(2)}, u32[]{:S(2)}) collective-permute-start(bf16[128,3712]{1,0:T(8,128)(2,1)S(1)} %pad_maximum_fusion.3), channel_id=1, source_target_pairs={{0,192},{1,49},{2,194},{3,51},{4,196},{5,53},{6,198},{7,55},{8,200... | collective-permute-start | bytes 2850824 | tf_op jit(solution)/shard_map/ppermute | solution.py:35
  70.5 17.2 %collective-permute-start.13 = (bf16[3584,512]{1,0:T(8,128)(2,1)S(1)}, bf16[3584,512]{1,0:T(8,128)(2,1)S(1)}, u32[]{:S(2)}, u32[]{:S(2)}) collective-permute-start(bf16[3584,512]{1,0:T(8,128)(2,1)S(1)} %pad_maximum_fusion.1), channel_id=1, source_target_pairs={{0,1},{1,0},{2,3},{3,2},{4,5},{5,4},{6,7},{7,6},{8,9},{9,8},{10,11... | collective-permute-start | bytes 11010056 | tf_op jit(solution)/shard_map/ppermute | solution.py:24
  72.3 13.7 %collective-permute-start.11 = (bf16[128,3712]{1,0:T(8,128)(2,1)S(1)}, bf16[128,3712]{1,0:T(8,128)(2,1)S(1)}, u32[]{:S(2)}, u32[]{:S(2)}) collective-permute-start(bf16[128,3712]{1,0:T(8,128)(2,1)S(1)} %collective-permute-done.7), channel_id=1, source_target_pairs={{0,64},{1,17},{2,66},{3,19},{4,68},{5,21},{6,70},{7,23},{8,72},{9,... | collective-permute-start | bytes 2850824 | tf_op jit(solution)/shard_map/ppermute | solution.py:35
  73.8 13.7 %collective-permute-start.12 = (bf16[128,3712]{1,0:T(8,128)(2,1)S(1)}, bf16[128,3712]{1,0:T(8,128)(2,1)S(1)}, u32[]{:S(2)}, u32[]{:S(2)}) collective-permute-start(bf16[128,3712]{1,0:T(8,128)(2,1)S(1)} %collective-permute-done.8), channel_id=1, source_target_pairs={{0,192},{1,49},{2,194},{3,51},{4,196},{5,53},{6,198},{7,55},{8,200... | collective-permute-start | bytes 2850824 | tf_op jit(solution)/shard_map/ppermute | solution.py:35
  90.7 5.9 %collective-permute-start.14 = (f32[768,512]{1,0:T(8,128)S(1)}, f32[768,512]{1,0:T(8,128)S(1)}, u32[]{:S(2)}, u32[]{:S(2)}) collective-permute-start(f32[768,512]{1,0:T(8,128)S(1)} %fusion), channel_id=1, source_target_pairs={{0,1},{1,0},{2,3},{3,2},{4,5},{5,4},{6,7},{7,6},{8,9},{9,8},{10,11... | collective-permute-start | bytes 4718600 | tf_op jit(solution)/shard_map/ppermute | solution.py:24
  91.9 4.7 %collective-permute-start.15 = (f32[256,512]{1,0:T(8,128)S(1)}, f32[256,512]{1,0:T(8,128)S(1)}, u32[]{:S(2)}, u32[]{:S(2)}) collective-permute-start(f32[256,512]{1,0:T(8,128)S(1)} %fusion.4), channel_id=1, source_target_pairs={{0,1},{1,0},{2,3},{3,2},{4,5},{5,4},{6,7},{7,6},{8,9},{9,8},{10,11... | collective-permute-start | bytes 1572872 | tf_op jit(solution)/shard_map/ppermute | solution.py:24
  98.2 2.0 %collective-permute-start.16 = (bf16[1024,256]{1,0:T(8,128)(2,1)S(1)}, bf16[1024,256]{1,0:T(8,128)(2,1)S(1)}, u32[]{:S(2)}, u32[]{:S(2)}) collective-permute-start(bf16[1024,256]{1,0:T(8,128)(2,1)S(1)} %get-tuple-element.74), channel_id=1, source_target_pairs={{0,1},{1,0},{2,3},{3,2},{4,5},{5,4},{6,7},{7,6},{8,9},{9,8},{10,11... | collective-permute-start | bytes 1572872 | tf_op jit(solution)/shard_map/ppermute | solution.py:24
  104.7 13.5 %collective-permute-start.18 = (bf16[128,3584]{1,0:T(8,128)(2,1)S(1)}, bf16[128,3584]{1,0:T(8,128)(2,1)S(1)}, u32[]{:S(2)}, u32[]{:S(2)}) collective-permute-start(bf16[128,3584]{1,0:T(8,128)(2,1)S(1)} %get-tuple-element.77), channel_id=1, source_target_pairs={{0,64},{1,17},{2,66},{3,19},{4,68},{5,21},{6,70},{7,23},{8,72},{9,... | collective-permute-start | bytes 2752520 | tf_op jit(solution)/shard_map/ppermute | solution.py:35
  106.0 14.0 %collective-permute-start.19 = (bf16[128,3584]{1,0:T(8,128)(2,1)S(1)}, bf16[128,3584]{1,0:T(8,128)(2,1)S(1)}, u32[]{:S(2)}, u32[]{:S(2)}) collective-permute-start(bf16[128,3584]{1,0:T(8,128)(2,1)S(1)} %get-tuple-element.76), channel_id=1, source_target_pairs={{0,192},{1,49},{2,194},{3,51},{4,196},{5,53},{6,198},{7,55},{8,200... | collective-permute-start | bytes 2752520 | tf_op jit(solution)/shard_map/ppermute | solution.py:35
  107.0 22.9 %collective-permute-start.17 = (bf16[128,3584]{1,0:T(8,128)(2,1)S(1)}, bf16[128,3584]{1,0:T(8,128)(2,1)S(1)}, u32[]{:S(2)}, u32[]{:S(2)}) collective-permute-start(bf16[128,3584]{1,0:T(8,128)(2,1)S(1)} %get-tuple-element.60), channel_id=1, source_target_pairs={{0,192},{1,49},{2,194},{3,51},{4,196},{5,53},{6,198},{7,55},{8,200... | collective-permute-start | bytes 2752520 | tf_op jit(solution)/shard_map/ppermute | solution.py:35
  109.8 20.1 %collective-permute-start.21 = (bf16[128,3584]{1,0:T(8,128)(2,1)S(1)}, bf16[128,3584]{1,0:T(8,128)(2,1)S(1)}, u32[]{:S(2)}, u32[]{:S(2)}) collective-permute-start(bf16[128,3584]{1,0:T(8,128)(2,1)S(1)} %get-tuple-element.61), channel_id=1, source_target_pairs={{0,64},{1,17},{2,66},{3,19},{4,68},{5,21},{6,70},{7,23},{8,72},{9,... | collective-permute-start | bytes 2752520 | tf_op jit(solution)/shard_map/ppermute | solution.py:35
  120.5 17.4 %collective-permute-start.20 = (bf16[128,3584]{1,0:T(8,128)(2,1)S(1)}, bf16[128,3584]{1,0:T(8,128)(2,1)S(1)}, u32[]{:S(2)}, u32[]{:S(2)}) collective-permute-start(bf16[128,3584]{1,0:T(8,128)(2,1)S(1)} %get-tuple-element.54), channel_id=1, source_target_pairs={{0,64},{1,17},{2,66},{3,19},{4,68},{5,21},{6,70},{7,23},{8,72},{9,... | collective-permute-start | bytes 2752520 | tf_op jit(solution)/shard_map/ppermute | solution.py:35
  122.6 17.1 %collective-permute-start.22 = (bf16[128,3584]{1,0:T(8,128)(2,1)S(1)}, bf16[128,3584]{1,0:T(8,128)(2,1)S(1)}, u32[]{:S(2)}, u32[]{:S(2)}) collective-permute-start(bf16[128,3584]{1,0:T(8,128)(2,1)S(1)} %get-tuple-element.55), channel_id=1, source_target_pairs={{0,192},{1,49},{2,194},{3,51},{4,196},{5,53},{6,198},{7,55},{8,200... | collective-permute-start | bytes 2752520 | tf_op jit(solution)/shard_map/ppermute | solution.py:35
  140.4 6.5 %collective-permute-start.25 = (bf16[32,3584]{1,0:T(8,128)(2,1)S(1)}, bf16[32,3584]{1,0:T(8,128)(2,1)S(1)}, u32[]{:S(2)}, u32[]{:S(2)}) collective-permute-start(bf16[32,3584]{1,0:T(8,128)(2,1)S(1)} %get-tuple-element.81), channel_id=1, source_target_pairs={{0,48},{1,193},{2,50},{3,195},{4,52},{5,197},{6,54},{7,199},{8,56}... | collective-permute-start | bytes 688136 | tf_op jit(solution)/shard_map/ppermute | solution.py:35
  143.4 7.2 %collective-permute-start.24 = (bf16[32,3584]{1,0:T(8,128)(2,1)S(1)}, bf16[32,3584]{1,0:T(8,128)(2,1)S(1)}, u32[]{:S(2)}, u32[]{:S(2)}) collective-permute-start(bf16[32,3584]{1,0:T(8,128)(2,1)S(1)} %get-tuple-element.82), channel_id=1, source_target_pairs={{0,16},{1,65},{2,18},{3,67},{4,20},{5,69},{6,22},{7,71},{8,24},{9,... | collective-permute-start | bytes 688136 | tf_op jit(solution)/shard_map/ppermute | solution.py:35
  143.4 10.6 %collective-permute-start.23 = (bf16[32,3584]{1,0:T(8,128)(2,1)S(1)}, bf16[32,3584]{1,0:T(8,128)(2,1)S(1)}, u32[]{:S(2)}, u32[]{:S(2)}) collective-permute-start(bf16[32,3584]{1,0:T(8,128)(2,1)S(1)} %get-tuple-element.80), channel_id=1, source_target_pairs={{0,48},{1,193},{2,50},{3,195},{4,52},{5,197},{6,54},{7,199},{8,56}... | collective-permute-start | bytes 688136 | tf_op jit(solution)/shard_map/ppermute | solution.py:35
  146.6 7.4 %collective-permute-start.27 = (bf16[32,3584]{1,0:T(8,128)(2,1)S(1)}, bf16[32,3584]{1,0:T(8,128)(2,1)S(1)}, u32[]{:S(2)}, u32[]{:S(2)}) collective-permute-start(bf16[32,3584]{1,0:T(8,128)(2,1)S(1)} %slice.203), channel_id=1, source_target_pairs={{0,16},{1,65},{2,18},{3,67},{4,20},{5,69},{6,22},{7,71},{8,24},{9,... | collective-permute-start | bytes 688136 | tf_op jit(solution)/shard_map/ppermute | solution.py:35
  150.7 7.3 %collective-permute-start.26 = (bf16[32,3584]{1,0:T(8,128)(2,1)S(1)}, bf16[32,3584]{1,0:T(8,128)(2,1)S(1)}, u32[]{:S(2)}, u32[]{:S(2)}) collective-permute-start(bf16[32,3584]{1,0:T(8,128)(2,1)S(1)} %add_convert_fusion.7), channel_id=1, source_target_pairs={{0,16},{1,65},{2,18},{3,67},{4,20},{5,69},{6,22},{7,71},{8,24},{9,... | collective-permute-start | bytes 688136 | tf_op jit(solution)/shard_map/ppermute | solution.py:35
  150.8 7.2 %collective-permute-start.28 = (bf16[32,3584]{1,0:T(8,128)(2,1)S(1)}, bf16[32,3584]{1,0:T(8,128)(2,1)S(1)}, u32[]{:S(2)}, u32[]{:S(2)}) collective-permute-start(bf16[32,3584]{1,0:T(8,128)(2,1)S(1)} %add_convert_fusion.6), channel_id=1, source_target_pairs={{0,48},{1,193},{2,50},{3,195},{4,52},{5,197},{6,54},{7,199},{8,56}... | collective-permute-start | bytes 688136 | tf_op jit(solution)/shard_map/ppermute | solution.py:35
